TPU v7x, 32 devices: a whole 2x2x4 slice. The times are simulated.
32 devices in a mesh: seq: 8 (over z, y), kv: 4 (over x, core).
Axes of the slice: x: 2, y: 2, z: 4, core: 2. Of those that a mesh axis runs over, the one named last changes fastest.
Arguments:
- tokens: bfloat16 [8192, 2048], P(('seq', 'kv')), may hold values from -6 to 6
- cotangent: bfloat16 [8192, 2048], P(('seq', 'kv')), may hold values from -6 to 6
- corpus_id: int32 [8], P('seq'), may hold values from 0 to 7
- corpus_weight: float32 [8], replicated, may hold values from 0.5 to 2
- step_count: int32 [1], replicated, may hold values from 1 to 20
- qkv_weight: float32 [2048, 1920], P(('seq', 'kv')), may hold values from -0.125 to 0.125
- out_weight: float32 [1280, 2048], P(('seq', 'kv')), may hold values from -1.25 to 1.25
- gains: float32 [4224], P(('seq', 'kv')), may hold values from 0.5 to 1.5
- gate_weight: float32 [2048, 5632], P('seq', 'kv'), may hold values from -0.125 to 0.125
- up_weight: float32 [2048, 5632], P('seq', 'kv'), may hold values from -0.125 to 0.125
- down_weight: float32 [2048, 5632], P('seq', 'kv'), may hold values from -0.078125 to 0.078125
- first_qkv: float32 [2048, 1920], P(('seq', 'kv')), may hold values from -64 to 64
- first_out: float32 [1280, 2048], P(('seq', 'kv')), may hold values from -8 to 8
- first_gains: float32 [4224], P(('seq', 'kv')), may hold values from -96 to 96
- first_gate: float32 [2048, 5632], P('seq', 'kv'), may hold values from -16 to 16
- first_up: float32 [2048, 5632], P('seq', 'kv'), may hold values from -16 to 16
- first_down: float32 [2048, 5632], P('seq', 'kv'), may hold values from -40 to 40
- second_qkv: float32 [2048, 1920], P(('seq', 'kv')), may hold values from 434.176 to 1720.32
- second_out: float32 [1280, 2048], P(('seq', 'kv')), may hold values from 9.8304 to 38.5024
- second_gains: float32 [4224], P(('seq', 'kv')), may hold values from 983.04 to 3850.24
- second_gate: float32 [2048, 5632], P('seq', 'kv'), may hold values from 39.3216 to 155.648
- second_up: float32 [2048, 5632], P('seq', 'kv'), may hold values from 39.3216 to 155.648
- second_down: float32 [2048, 5632], P('seq', 'kv'), may hold values from 212.992 to 819.2
Outputs:
- block_out: bfloat16 [8192, 2048], P(('seq', 'kv'))
- grad_input: float32 [8192, 2048], P(('seq', 'kv'))
- new_qkv: float32 [2048, 1920], P(('seq', 'kv'))
- moments_qkv: float32 [2, 2048, 1920], P(None, ('seq', 'kv'))
- new_out: float32 [1280, 2048], P(('seq', 'kv'))
- moments_out: float32 [2, 1280, 2048], P(None, ('seq', 'kv'))
- new_gains: float32 [4224], P(('seq', 'kv'))
- moments_gains: float32 [2, 4224], P(None, ('seq', 'kv'))
- new_gate: float32 [2048, 5632], P('seq', 'kv')
- moments_gate: float32 [2, 2048, 5632], P(None, 'seq', 'kv')
- new_up: float32 [2048, 5632], P('seq', 'kv')
- moments_up: float32 [2, 2048, 5632], P(None, 'seq', 'kv')
- new_down: float32 [2048, 5632], P('seq', 'kv')
- moments_down: float32 [2, 2048, 5632], P(None, 'seq', 'kv')
All inputs are finite; a program needn't handle non-finite values.
Results may differ from a plain program's by a relative error of at most 0.014.
The roundings to bfloat16 on the way count: a program that leaves them out, or rounds other values in their place, can miss the bound.
Values may be sent and summed in bfloat16 or wider, within the bound.
No kernel may reach another device: no remote copies, remote signals or barrier semaphores. Data moves between devices by JAX's collectives and lax.ppermute only.
A program may use at most 256 MiB of HBM per device.

v0:
```python
import jax
import jax.numpy as jnp
import numpy as np
from jax import lax
from jax.sharding import PartitionSpec as P

QUERY_HEADS = 20
VALUE_GROUPS = 5
HEAD_SIZE = 64


eps_norm = 1e-06
masked_value = -1e30
beta_first = 0.9
beta_second = 0.95
adam_eps = 1e-08
slot_groups = np.array([[0, 1], [2, 5], [3, 5], [4, 5]])
group_home = np.array([0, 0, 1, 2, 3])
group_slot = np.array([0, 1, 0, 0, 0])


def rms_scale(value_rows):
    return lax.rsqrt(jnp.mean(value_rows * value_rows, -1, keepdims=True) + eps_norm)


def norm_back(grad_out, value_rows, scale, gain):
    shaped = value_rows * scale
    pushed = grad_out * gain
    grad_in = scale * (pushed - shaped * jnp.mean(pushed * shaped, -1, keepdims=True))
    return (grad_in, grad_out * shaped)


def angle_tables(item_count, offset, model_width):
    places = (jnp.arange(item_count) + offset).astype(jnp.float32)
    freqs = 10000.0 ** (-(jnp.arange(model_width // 2).astype(jnp.float32) * 2.0 / model_width))
    angles = places[:, None] * freqs[None, :]
    angles = jnp.concatenate([angles, angles], axis=-1)
    return (jnp.cos(angles)[:, None, :], jnp.sin(angles)[:, None, :])


def rotate(value_rows, cosine, sine):
    half = value_rows.shape[-1] // 2
    turned = jnp.concatenate([-value_rows[..., half:], value_rows[..., :half]], axis=-1)
    return value_rows * cosine + turned * sine


def turn_back(grads, cosine, sine):
    half = grads.shape[-1] // 2
    moved = grads * sine
    return grads * cosine + jnp.concatenate([moved[..., half:], -moved[..., :half]], axis=-1)


def into_group_slots(per_group):
    item_count = per_group.shape[0]
    padded = jnp.concatenate([per_group, jnp.zeros_like(per_group[:, :1])], axis=1)
    placed = padded[:, slot_groups]
    return placed.reshape(item_count, slot_groups.shape[0], -1)


def from_slots(received, model_width):
    item_count = received.shape[0]
    shaped = received.reshape(item_count, slot_groups.shape[0], 2, model_width)
    return shaped[:, group_home, group_slot]


def project(tokens, gain_values, mixer_full, cosine, sine):
    item_count, model = tokens.shape
    inputs = tokens.astype(jnp.float32)
    scale_one = rms_scale(inputs)
    normed = (inputs * scale_one * gain_values[:model]).astype(jnp.bfloat16)
    mixed_output = jnp.dot(normed, mixer_full, preferred_element_type=jnp.float32)
    queries = mixed_output[:, : QUERY_HEADS * HEAD_SIZE].reshape(item_count, QUERY_HEADS, HEAD_SIZE)
    key_rows = mixed_output[
        :, QUERY_HEADS * HEAD_SIZE : (QUERY_HEADS + VALUE_GROUPS) * HEAD_SIZE
    ].reshape(item_count, VALUE_GROUPS, HEAD_SIZE)
    value_rows = mixed_output[:, (QUERY_HEADS + VALUE_GROUPS) * HEAD_SIZE :].reshape(
        item_count, VALUE_GROUPS, HEAD_SIZE
    )
    scale_q = rms_scale(queries)
    scale_k = rms_scale(key_rows)
    rotated_query = rotate(
        queries * scale_q * gain_values[2 * model : 2 * model + HEAD_SIZE], cosine, sine
    ).astype(jnp.bfloat16)
    rotated_key = rotate(
        key_rows * scale_k * gain_values[2 * model + HEAD_SIZE :], cosine, sine
    ).astype(jnp.bfloat16)
    grouped_rows = jnp.concatenate(
        [
            rotated_query.reshape(item_count, VALUE_GROUPS, -1),
            rotated_key,
            value_rows.astype(jnp.bfloat16),
        ],
        axis=-1,
    )
    return (
        inputs,
        scale_one,
        normed,
        queries,
        key_rows,
        scale_q,
        scale_k,
        into_group_slots(grouped_rows),
    )


def split_slot(slot):
    token_length = slot.shape[0]
    model_width = QUERY_HEADS // VALUE_GROUPS
    queries = slot[:, : model_width * HEAD_SIZE].reshape(token_length, model_width, HEAD_SIZE)
    key_rows = slot[:, model_width * HEAD_SIZE : (model_width + 1) * HEAD_SIZE]
    value_rows = slot[:, (model_width + 1) * HEAD_SIZE :]
    return (queries, key_rows, value_rows)


def block_scores(part, key_rows, start, block, token_length):
    scores = jnp.einsum("qhd,kd->hqk", part, key_rows, preferred_element_type=jnp.float32) * 0.125
    allowed = jnp.arange(token_length)[None, :] <= (start + jnp.arange(block))[:, None]
    return jnp.where(allowed[None], scores, masked_value)


def slot_forward(slot):
    token_length = slot.shape[0]
    model_width = QUERY_HEADS // VALUE_GROUPS
    block = min(512, token_length)
    queries, key_rows, value_rows = split_slot(slot)

    def one_block(index):
        start = index * block
        part = lax.dynamic_slice_in_dim(queries, start, block, 0)
        scores = block_scores(part, key_rows, start, block, token_length)
        top = jnp.max(scores, -1, keepdims=True)
        weights = jnp.exp(scores - top)
        total = jnp.sum(weights, -1, keepdims=True)
        probs = (weights / total).astype(jnp.bfloat16)
        result = jnp.einsum("hqk,kd->qhd", probs, value_rows, preferred_element_type=jnp.float32)
        return (
            result.astype(jnp.bfloat16).reshape(block, model_width * HEAD_SIZE),
            (top + jnp.log(total))[..., 0],
        )

    results, sums_log = lax.map(one_block, jnp.arange(token_length // block))
    return (results.reshape(token_length, model_width * HEAD_SIZE), sums_log)


def slot_backward(slot, grad_slot, sums_log):
    token_length = slot.shape[0]
    model_width = QUERY_HEADS // VALUE_GROUPS
    block = min(512, token_length)
    queries, key_rows, value_rows = split_slot(slot)
    grads_out = grad_slot.reshape(token_length, model_width, HEAD_SIZE)

    def one_block(carry, index):
        grad_keys, grad_values = carry
        start = index * block
        part = lax.dynamic_slice_in_dim(queries, start, block, 0)
        grad_part = lax.dynamic_slice_in_dim(grads_out, start, block, 0)
        scores = block_scores(part, key_rows, start, block, token_length)
        probs = jnp.exp(scores - sums_log[index][..., None])
        grad_probs = jnp.einsum(
            "qhd,kd->hqk", grad_part, value_rows, preferred_element_type=jnp.float32
        )
        inner = jnp.sum(probs * grad_probs, -1, keepdims=True)
        grad_scores = (probs * (grad_probs - inner)).astype(jnp.bfloat16)
        grad_queries = (
            jnp.einsum("hqk,kd->qhd", grad_scores, key_rows, preferred_element_type=jnp.float32)
            * 0.125
        )
        grad_keys = (
            grad_keys
            + jnp.einsum("hqk,qhd->kd", grad_scores, part, preferred_element_type=jnp.float32)
            * 0.125
        )
        grad_values = grad_values + jnp.einsum(
            "hqk,qhd->kd", probs.astype(jnp.bfloat16), grad_part, preferred_element_type=jnp.float32
        )
        return ((grad_keys, grad_values), grad_queries.reshape(block, model_width * HEAD_SIZE))

    empty = jnp.zeros((token_length, HEAD_SIZE), jnp.float32)
    (grad_keys, grad_values), grad_queries = lax.scan(
        one_block, (empty, empty), jnp.arange(token_length // block)
    )
    joined = jnp.concatenate(
        [grad_queries.reshape(token_length, model_width * HEAD_SIZE), grad_keys, grad_values],
        axis=-1,
    )
    return joined.astype(jnp.bfloat16)


def send_ffn(ffn_terms):
    return (
        lax.psum_scatter(
            ffn_terms[0].astype(jnp.bfloat16), "seq", scatter_dimension=0, tiled=True
        ).astype(jnp.float32),
        lax.psum_scatter(
            ffn_terms[1].astype(jnp.bfloat16), "seq", scatter_dimension=0, tiled=True
        ).astype(jnp.float32),
        lax.psum_scatter(
            ffn_terms[2].astype(jnp.bfloat16), "seq", scatter_dimension=0, tiled=True
        ).astype(jnp.float32),
    )


def adamw(weight, grad, first, second, rate, shrink, item_count):
    first_new = beta_first * first + (1.0 - beta_first) * grad
    second_new = beta_second * second + (1.0 - beta_second) * grad * grad
    fix_first = 1.0 - jnp.power(beta_first, item_count)
    fix_second = 1.0 - jnp.power(beta_second, item_count)
    stepped = first_new / fix_first / (jnp.sqrt(second_new / fix_second) + adam_eps)
    return (
        weight - rate * (stepped + shrink * weight),
        jnp.stack([first_new, jnp.sqrt(second_new)]),
    )


def contract_rows(left, right):
    return lax.dot_general(
        left, right, (((0,), (0,)), ((), ())), preferred_element_type=jnp.float32
    )


def contract_cols(left, right):
    return lax.dot_general(
        left, right, (((1,), (1,)), ((), ())), preferred_element_type=jnp.float32
    )


def local(
    tokens,
    cotangent,
    corpus_id,
    corpus_weight,
    step_count,
    qkv_weight,
    out_weight,
    gains,
    gate_weight,
    up_weight,
    down_weight,
    first_qkv,
    first_out,
    first_gains,
    first_gate,
    first_up,
    first_down,
    second_qkv,
    second_out,
    second_gains,
    second_gate,
    second_up,
    second_down,
):
    mixer_full, output_full, gains_low = (
        lax.all_gather(qkv_weight.astype(jnp.bfloat16), ("seq", "kv"), axis=0, tiled=True),
        lax.all_gather(out_weight.astype(jnp.bfloat16), ("seq", "kv"), axis=0, tiled=True),
        lax.all_gather(gains.astype(jnp.bfloat16), ("seq", "kv"), axis=0, tiled=True),
    )
    gate_full, up_full, down_full = (
        lax.all_gather(gate_weight.astype(jnp.bfloat16), "seq", axis=0, tiled=True),
        lax.all_gather(up_weight.astype(jnp.bfloat16), "seq", axis=0, tiled=True),
        lax.all_gather(down_weight.astype(jnp.bfloat16), "seq", axis=0, tiled=True),
    )
    item_count, model = tokens.shape
    gain_values = gains_low.astype(jnp.float32)
    head_width_size = QUERY_HEADS // VALUE_GROUPS * HEAD_SIZE
    cosine, sine = angle_tables(item_count, lax.axis_index("kv") * item_count, HEAD_SIZE)
    is_double = lax.axis_index("kv") == 0
    inputs, scale_one, normed, queries, key_rows, scale_q, scale_k, outgoing = project(
        tokens, gain_values, mixer_full, cosine, sine
    )
    grouped_rows = lax.all_to_all(outgoing, "kv", split_axis=1, concat_axis=0, tiled=True)
    token_length = grouped_rows.shape[0]
    grouped_rows = grouped_rows.reshape(token_length, 2, -1)
    first_result, first_log = slot_forward(grouped_rows[:, 0])
    second_result, second_log = lax.cond(
        is_double,
        lambda: slot_forward(grouped_rows[:, 1]),
        lambda: (jnp.zeros_like(first_result), jnp.zeros_like(first_log)),
    )
    results = jnp.stack([first_result, second_result], 1).reshape(token_length, -1)
    returned = lax.all_to_all(results, "kv", split_axis=0, concat_axis=1, tiled=True)
    attended = from_slots(returned, head_width_size).reshape(item_count, QUERY_HEADS * HEAD_SIZE)
    hidden = inputs + jnp.dot(attended, output_full, preferred_element_type=jnp.float32)
    scale_two = rms_scale(hidden)
    gain_two = gain_values[model : 2 * model]
    normed_two = (hidden * scale_two * gain_two).astype(jnp.bfloat16)
    ffn_rows = lax.all_gather(normed_two, "kv", axis=0, tiled=True)
    gate = jnp.dot(ffn_rows, gate_full, preferred_element_type=jnp.float32)
    up_part = jnp.dot(ffn_rows, up_full, preferred_element_type=jnp.float32)
    sigma = jax.nn.sigmoid(gate)
    swish = gate * sigma
    acted = (swish * up_part).astype(jnp.bfloat16)
    partial_out = contract_cols(acted, down_full)
    ffn = lax.psum_scatter(
        partial_out.astype(jnp.bfloat16), "kv", scatter_dimension=0, tiled=True
    ).astype(jnp.float32)
    block_out = (hidden + ffn).astype(jnp.bfloat16)
    factor = jnp.sum(
        jnp.where(jnp.arange(corpus_weight.shape[0]) == corpus_id[0], corpus_weight, 0.0)
    )
    weighted = cotangent.astype(jnp.float32) * factor
    weighted_rows = lax.all_gather(weighted.astype(jnp.bfloat16), "kv", axis=0, tiled=True)
    grad_acted = jnp.dot(weighted_rows, down_full, preferred_element_type=jnp.float32)
    grad_down = contract_rows(weighted_rows, acted)
    grad_gate = (grad_acted * up_part * sigma * (1.0 + gate * (1.0 - sigma))).astype(jnp.bfloat16)
    grad_up = (grad_acted * swish).astype(jnp.bfloat16)
    ffn_terms = (contract_rows(ffn_rows, grad_gate), contract_rows(ffn_rows, grad_up), grad_down)
    grad_rows = contract_cols(grad_gate, gate_full) + contract_cols(grad_up, up_full)
    grad_normed_two = lax.psum_scatter(
        grad_rows.astype(jnp.bfloat16), "kv", scatter_dimension=0, tiled=True
    ).astype(jnp.float32)
    pushed_two, gain_two_terms = norm_back(grad_normed_two, hidden, scale_two, gain_two)
    grad_hidden = weighted + pushed_two
    hidden_low = grad_hidden.astype(jnp.bfloat16)
    grad_output = contract_rows(attended, hidden_low)
    attended_gradient = contract_cols(hidden_low, output_full).astype(jnp.bfloat16)
    outgoing_gradient = into_group_slots(
        attended_gradient.reshape(item_count, VALUE_GROUPS, head_width_size)
    )
    grad_grouped = lax.all_to_all(
        outgoing_gradient, "kv", split_axis=1, concat_axis=0, tiled=True
    ).reshape(token_length, 2, -1)
    inputs, scale_one, normed, queries, key_rows, scale_q, scale_k, outgoing = project(
        tokens, gain_values, mixer_full, cosine, sine
    )
    regrouped = lax.all_to_all(outgoing, "kv", split_axis=1, concat_axis=0, tiled=True).reshape(
        token_length, 2, -1
    )
    first_back = slot_backward(regrouped[:, 0], grad_grouped[:, 0], first_log)
    second_back = lax.cond(
        is_double,
        lambda: slot_backward(regrouped[:, 1], grad_grouped[:, 1], second_log),
        lambda: jnp.zeros_like(first_back),
    )
    backs = jnp.stack([first_back, second_back], 1).reshape(token_length, -1)
    arrived = lax.all_to_all(backs, "kv", split_axis=0, concat_axis=1, tiled=True)
    per_group = from_slots(arrived, head_width_size + 2 * HEAD_SIZE).astype(jnp.float32)
    grad_turned_q = per_group[..., :head_width_size].reshape(item_count, QUERY_HEADS, HEAD_SIZE)
    grad_turned_k = per_group[..., head_width_size : head_width_size + HEAD_SIZE]
    grad_values = per_group[..., head_width_size + HEAD_SIZE :]
    grad_queries, gain_q_terms = norm_back(
        turn_back(grad_turned_q, cosine, sine),
        queries,
        scale_q,
        gain_values[2 * model : 2 * model + HEAD_SIZE],
    )
    grad_keys, gain_k_terms = norm_back(
        turn_back(grad_turned_k, cosine, sine),
        key_rows,
        scale_k,
        gain_values[2 * model + HEAD_SIZE :],
    )
    grad_mixed = jnp.concatenate(
        [
            grad_queries.reshape(item_count, -1),
            grad_keys.reshape(item_count, -1),
            grad_values.reshape(item_count, -1),
        ],
        axis=-1,
    ).astype(jnp.bfloat16)
    grad_mixer = contract_rows(normed, grad_mixed)
    grad_normed = contract_cols(grad_mixed, mixer_full)
    pushed_one, gain_one_terms = norm_back(grad_normed, inputs, scale_one, gain_values[:model])
    grad_input = grad_hidden + pushed_one
    grad_gains = jnp.concatenate(
        [
            jnp.sum(gain_one_terms, 0),
            jnp.sum(gain_two_terms, 0),
            jnp.sum(gain_q_terms, (0, 1)),
            jnp.sum(gain_k_terms, (0, 1)),
        ]
    )
    attn_shares = (
        lax.psum_scatter(grad_mixer, ("seq", "kv"), scatter_dimension=0, tiled=True),
        lax.psum_scatter(grad_output, ("seq", "kv"), scatter_dimension=0, tiled=True),
        lax.psum_scatter(grad_gains, ("seq", "kv"), scatter_dimension=0, tiled=True),
    )
    ffn_shares = send_ffn(ffn_terms)
    steps_done = step_count[0].astype(jnp.float32)
    new_qkv, moments_qkv = adamw(
        qkv_weight, attn_shares[0], first_qkv, second_qkv, 0.02, 0.1, steps_done
    )
    new_out, moments_out = adamw(
        out_weight, attn_shares[1], first_out, second_out, 0.2, 0.1, steps_done
    )
    new_gains, moments_gains = adamw(
        gains, attn_shares[2], first_gains, second_gains, 0.6, 0.0, steps_done
    )
    new_gate, moments_gate = adamw(
        gate_weight, ffn_shares[0], first_gate, second_gate, 0.02, 0.1, steps_done
    )
    new_up, moments_up = adamw(up_weight, ffn_shares[1], first_up, second_up, 0.02, 0.1, steps_done)
    new_down, moments_down = adamw(
        down_weight, ffn_shares[2], first_down, second_down, 0.013, 0.1, steps_done
    )
    return (
        block_out,
        grad_input,
        new_qkv,
        moments_qkv,
        new_out,
        moments_out,
        new_gains,
        moments_gains,
        new_gate,
        moments_gate,
        new_up,
        moments_up,
        new_down,
        moments_down,
    )


def solution(mesh):
    return jax.shard_map(
        local,
        mesh=mesh,
        in_specs=(
            P(("seq", "kv"), None),
            P(("seq", "kv"), None),
            P("seq"),
            P(),
            P(),
            P(("seq", "kv"), None),
            P(("seq", "kv"), None),
            P(("seq", "kv")),
            P("seq", "kv"),
            P("seq", "kv"),
            P("seq", "kv"),
            P(("seq", "kv"), None),
            P(("seq", "kv"), None),
            P(("seq", "kv")),
            P("seq", "kv"),
            P("seq", "kv"),
            P("seq", "kv"),
            P(("seq", "kv"), None),
            P(("seq", "kv"), None),
            P(("seq", "kv")),
            P("seq", "kv"),
            P("seq", "kv"),
            P("seq", "kv"),
        ),
        out_specs=(
            P(("seq", "kv"), None),
            P(("seq", "kv"), None),
            P(("seq", "kv"), None),
            P(None, ("seq", "kv"), None),
            P(("seq", "kv"), None),
            P(None, ("seq", "kv"), None),
            P(("seq", "kv")),
            P(None, ("seq", "kv")),
            P("seq", "kv"),
            P(None, "seq", "kv"),
            P("seq", "kv"),
            P(None, "seq", "kv"),
            P("seq", "kv"),
            P(None, "seq", "kv"),
        ),
        check_vma=False,
    )
```

profile of v0, /device:TPU:0, one launch (start us, length us, event | category | flops | bytes accessed | tf_op | source)
XLA Modules:
  0.0 1318.3 jit_solution(16976503821957024039)
XLA Ops:
  12.2 42.7 %all-reduce.2 = bf16[4224]{0:T(1024)(128)(2,1)S(1)} all-reduce(bf16[4224]{0:T(1024)(128)(2,1)S(1)} %dynamic-update-slice), channel_id=1, replica_groups=mesh['seq'=8,'kv'=4] {'seq','kv'}, use_global_device_ids=true, to_apply=%add.2 | all-reduce | flops 4224 | bytes 16896
  59.8 30.2 %all-gather.8.cloned.1.call-done = bf16[2048,1920]{1,0:T(8,128)(2,1)} async-done(((bf16[64,1920]{1,0:T(8,128)(2,1)}), bf16[2048,1920]{1,0:T(8,128)(2,1)}) %all-gather.8.cloned.1.call-update) | async-done | bytes 7864336 | tf_op jit(solution)/shard_map/all_gather | solution.py:254
  117.9 23.2 %all-to-all-done = bf16[256,4,768]{0,2,1:T(8,128)(2,1)S(1)} async-done(((bf16[256,4,768]{0,2,1:T(8,128)(2,1)}), bf16[256,4,768]{0,2,1:T(8,128)(2,1)S(1)}, u32[]{:S(2)}, u32[]{:S(2)}) %all-to-all-start) | async-done | bytes 1572896 | tf_op jit(solution)/shard_map/all_to_all | solution.py:271
  147.3 25.6 %conditional.2 = (f32[2,4,512]{2,1,0:T(4,128)}, bf16[1024,1,256]{2,0,1:T(8,128)(2,1)}) conditional(s32[]{:T(128)} %convert_element_type.180, () %tuple.43, (bf16[1024,2,384]{2,1,0:T(2,128)(2,1)S(1)}) %tuple.68), branch_computations={%region_7.8_spmd, %region_8.13_spmd} | conditional | flops 562690560 | bytes 35459384 | solution.py:275
  152.0 20.5 %while.52 = (s32[]{:T(128)}, bf16[2,512,256]{2,1,0:T(8,128)(2,1)}, f32[2,4,512]{2,1,0:T(4,128)}, s32[2]{0:T(128)S(1)}, bf16[1024,4,64]{0,2,1:T(8,128)(2,1)S(1)},...) while((s32[]{:T(128)}, bf16[2,512,256]{2,1,0:T(8,128)(2,1)}, ...), condition=%wide.region_12.12_spmd, body=%wide.region_9.11_spmd.sunk | while | flops 562690560 | bytes 29167808 | solution.py:142
  172.9 17.9 %while.54 = (s32[]{:T(128)}, bf16[2,512,256]{2,1,0:T(8,128)(2,1)S(1)}, f32[2,4,512]{2,1,0:T(4,128)S(1)}, s32[2]{0:T(128)S(1)}, bf16[1024,4,64]{0,2,1:T(8,128)(2,...) while((s32[]{:T(128)}, ...), condition=%wide.region_6.7_spmd, body=%wide.region_3.6_spmd.sunk | while | flops 562690560 | bytes 29167808 | solution.py:142
  194.1 16.9 %all_to_all.76 = bf16[4,256,512]{2,1,0:T(8,128)(2,1)S(1)} all-to-all(bf16[4,256,512]{2,1,0:T(8,128)(2,1)S(1)} %all_to_all.60), channel_id=1, replica_groups=mesh['seq'=8,'kv'=4] {'kv'}, dimensions={0} | all-to-all | bytes 2097152 | tf_op jit(solution)/shard_map/all_to_all | solution.py:281
  228.7 26.3 %all-gather.14.cloned.1.call-done = bf16[2048,1408]{1,0:T(8,128)(2,1)} async-done(((bf16[256,1408]{1,0:T(8,128)(2,1)}), bf16[2048,1408]{1,0:T(8,128)(2,1)}) %all-gather.14.cloned.1.call-update) | async-done | bytes 5767184 | tf_op jit(solution)/shard_map/all_gather | solution.py:259
  255.0 34.7 %all-gather.12.cloned.1.call-done = bf16[1024,2048]{1,0:T(8,128)(2,1)} async-done(((bf16[256,2048]{1,0:T(8,128)(2,1)}), bf16[1024,2048]{1,0:T(8,128)(2,1)}) %all-gather.12.cloned.1.call-update) | async-done | bytes 4194320 | tf_op jit(solution)/shard_map/all_gather | solution.py:287
  289.6 11.7 fusion.142
  301.3 83.6 %all-gather.16.cloned.1.call-done = bf16[2048,1408]{1,0:T(8,128)(2,1)} async-done(((bf16[256,1408]{1,0:T(8,128)(2,1)}), bf16[2048,1408]{1,0:T(8,128)(2,1)}) %all-gather.16.cloned.1.call-update) | async-done | bytes 5767184 | tf_op jit(solution)/shard_map/all_gather | solution.py:260
  396.6 23.0 %all-gather.20.cloned.1.call-done = bf16[1024,2048]{1,0:T(8,128)(2,1)} async-done(((bf16[256,2048]{1,0:T(8,128)(2,1)}), bf16[1024,2048]{1,0:T(8,128)(2,1)}) %all-gather.20.cloned.1.call-update) | async-done | bytes 4194320 | tf_op jit(solution)/shard_map/all_gather | solution.py:302
  419.6 95.4 %all-gather.18.cloned.1.call-done = bf16[2048,1408]{1,0:T(8,128)(2,1)} async-done(((bf16[256,1408]{1,0:T(8,128)(2,1)}), bf16[2048,1408]{1,0:T(8,128)(2,1)}) %all-gather.18.cloned.1.call-update) | async-done | bytes 5767184 | tf_op jit(solution)/shard_map/all_gather | solution.py:261
  515.0 15.5 %multiply_convert_fusion = (bf16[1024,1408]{1,0:T(8,128)(2,1)S(1)}, bf16[1024,1408]{1,0:T(8,128)(2,1)S(1)}, bf16[1024,1408]{1,0:T(8,128)(2,1)}) fusion(f32[1024,1408]{1,0:T(8,128)} %fusion.142, f32[1024,1408]{1,0:T(8,128)} %fusion.143, bf16[1024,2048]{1,0:T(8,128)(2,1)} %all-gather.20.cloned.1.call-done, bf16[2048,1408]{1,0:T(8,128)(2,1)} %all-gather.18.cloned.1.call-done), kind=kOutput, calls=%fused_computation.121 | convolution fusion | flops 5927206912 | bytes 30146560 | tf_op jit(solution)/shard_map/dot_general | solution.py:303
  597.1 42.7 %reduce-scatter.8.cloned.1.call-done = bf16[256,2048]{1,0:T(8,128)(2,1)} async-done(((bf16[1024,2048]{1,0:T(8,128)(2,1)}), bf16[256,2048]{1,0:T(8,128)(2,1)}) %reduce-scatter.8.cloned.1.call-update) | async-done | bytes 1048592 | tf_op jit(solution)/shard_map/reduce_scatter | solution.py:294
  662.9 14.4 %all-to-all-done.2 = bf16[256,4,512]{0,2,1:T(8,128)(2,1)S(1)} async-done(((bf16[256,4,512]{0,2,1:T(8,128)(2,1)}), bf16[256,4,512]{0,2,1:T(8,128)(2,1)S(1)}, u32[]{:S(2)}, u32[]{:S(2)}) %all-to-all-start.2) | async-done | bytes 1048608 | tf_op jit(solution)/shard_map/all_to_all | solution.py:320
  679.6 57.1 %while.55 = (s32[]{:T(128)}, f32[1024,64]{0,1:T(8,128)S(1)}, f32[1024,64]{0,1:T(8,128)}, bf16[2,512,256]{2,1,0:T(8,128)(2,1)}, s32[2]{0:T(128)S(1)}, /*index=5*/...) while((s32[]{:T(128)}, f32[1024,64]{0,1:T(8,128)S(1)}, ...), condition=%wide.region_20.21_spmd.clone, body=%wide.region_18.20_spmd.clone.sunk | while | flops 1374747136 | bytes 112980416 | solution.py:180
  739.3 67.6 %conditional.3 = (bf16[1024,1,384]{2,0,1:T(8,128)(2,1)S(1)}) conditional(s32[]{:T(128)} %convert_element_type.180, () %tuple.45, (bf16[1024,2,384]{2,1,0:T(2,128)(2,1)S(1)}, bf16[1024,2,256]{2,1,0:T(2,128)(2,1)}, f32[2,4,512]{2,1,0:T(4,128)}) %tuple.196), branch_computations={%region_21.22_spmd, %region_22.26_spmd} | conditional | flops 1377237504 | bytes 129430064 | solution.py:330
  748.2 56.6 %while.53 = (s32[]{:T(128)}, f32[1024,64]{0,1:T(8,128)S(1)}, f32[1024,64]{0,1:T(8,128)S(1)}, bf16[2,512,256]{2,1,0:T(8,128)(2,1)S(1)}, s32[2]{0:T(128)S(1)}, /*i...) while((s32[]{:T(128)}, f32[1024,64]{0,1:T(8,128)S(1)}, ...), condition=%wide.region_25.25_spmd.clone, body=%wide.region_23.24_spmd.clone.sunk | while | flops 1374747136 | bytes 110817648 | solution.py:180
  819.6 16.9 %all-to-all-done.3 = bf16[4,256,768]{2,1,0:T(8,128)(2,1)} async-done(((bf16[4,256,768]{2,1,0:T(8,128)(2,1)}), bf16[4,256,768]{2,1,0:T(8,128)(2,1)}, u32[]{:S(2)}, u32[]{:S(2)}) %all-to-all-start.3) | async-done | bytes 1572896 | tf_op jit(solution)/shard_map/all_to_all | solution.py:336
  896.8 41.9 %all-reduce.3 = f32[4224]{0:T(1024)S(1)} all-reduce(f32[4224]{0:T(1024)S(1)} %concatenate.102), channel_id=6, replica_groups=mesh['seq'=8,'kv'=4] {'seq','kv'}, use_global_device_ids=true, to_apply=%region_36.37.clone | all-reduce | flops 4224 | bytes 33792
  957.2 23.6 %reduce-scatter.20.cloned.1.call-done = bf16[256,1408]{1,0:T(8,128)(2,1)} async-done(((bf16[2048,1408]{1,0:T(8,128)(2,1)}), bf16[256,1408]{1,0:T(8,128)(2,1)}) %reduce-scatter.20.cloned.1.call-update) | async-done | bytes 720912 | tf_op jit(solution)/shard_map/reduce_scatter | solution.py:198
  986.8 149.2 %reduce-scatter.14.cloned.1.call-done = f32[40,2048]{1,0:T(8,128)} async-done(((f32[1280,2048]{1,0:T(8,128)}), f32[40,2048]{1,0:T(8,128)}) %reduce-scatter.14.cloned.1.call-update) | async-done | bytes 327696 | tf_op jit(solution)/shard_map/reduce_scatter | solution.py:375
  1138.9 169.3 %reduce-scatter.12.cloned.1.call-done = f32[64,1920]{1,0:T(8,128)} async-done(((f32[2048,1920]{1,0:T(8,128)}), f32[64,1920]{1,0:T(8,128)}) %reduce-scatter.12.cloned.1.call-update) | async-done | bytes 491536 | tf_op jit(solution)/shard_map/reduce_scatter | solution.py:374
  (504 shorter events, 425.6 us)
Async XLA Ops:
  7.2 82.7 %all-gather.8.cloned.1.call-start = ((), (), s32[]{:S(2)}) async-start(), calls=%async_computation.11 | async-start | bytes 8110080 | tf_op jit(solution)/shard_map/all_gather | solution.py:254
  9.1 206.7 %all-gather.10.cloned.1.call-start = ((), (), s32[]{:S(2)}) async-start(), calls=%async_computation.12 | async-start | bytes 5406720 | tf_op jit(solution)/shard_map/all_gather | solution.py:255
  10.9 244.0 %all-gather.14.cloned.1.call-start = ((), (), s32[]{:S(2)}) async-start(), calls=%async_computation.14 | async-start | bytes 6488064 | tf_op jit(solution)/shard_map/all_gather | solution.py:259
  114.0 27.1 %all-to-all-start = ((bf16[256,4,768]{0,2,1:T(8,128)(2,1)}), bf16[256,4,768]{0,2,1:T(8,128)(2,1)S(1)}, u32[]{:S(2)}, u32[]{:S(2)}) async-start(bf16[256,4,768]{0,2,1:T(8,128)(2,1)} %bitcast.32), calls=%async_computation | async-start | bytes 3145728 | tf_op jit(solution)/shard_map/all_to_all | solution.py:271
  117.6 172.0 %all-gather.12.cloned.1.call-start = ((), (), s32[]{:S(2)}) async-start(), calls=%async_computation.13 | async-start | bytes 5242880 | tf_op jit(solution)/shard_map/all_gather | solution.py:287
  221.5 163.4 %all-gather.16.cloned.1.call-start = ((), (), s32[]{:S(2)}) async-start(), calls=%async_computation.15 | async-start | bytes 6488064 | tf_op jit(solution)/shard_map/all_gather | solution.py:260
  222.9 196.7 %all-gather.20.cloned.1.call-start = ((), (), s32[]{:S(2)}) async-start(), calls=%async_computation.18 | async-start | bytes 5242880 | tf_op jit(solution)/shard_map/all_gather | solution.py:302
  227.4 287.6 %all-gather.18.cloned.1.call-start = ((), (), s32[]{:S(2)}) async-start(), calls=%async_computation.16 | async-start | bytes 6488064 | tf_op jit(solution)/shard_map/all_gather | solution.py:261
  228.5 366.1 %reduce-scatter.10.cloned.1.call-start = ((), (), s32[]{:S(2)}) async-start(), calls=%async_computation.19 | async-start | bytes 5242880 | tf_op jit(solution)/shard_map/reduce_scatter | solution.py:309
  549.7 90.1 %reduce-scatter.8.cloned.1.call-start = ((), (), s32[]{:S(2)}) async-start(), calls=%async_computation.17 | async-start | bytes 5242880 | tf_op jit(solution)/shard_map/reduce_scatter | solution.py:294
  561.2 382.3 %reduce-scatter.16.cloned.1.call-start = ((), (), s32[]{:S(2)}) async-start(), calls=%async_computation.22 | async-start | bytes 6488064 | tf_op jit(solution)/shard_map/reduce_scatter | solution.py:192
  572.2 378.1 %reduce-scatter.18.cloned.1.call-start = ((), (), s32[]{:S(2)}) async-start(), calls=%async_computation.23 | async-start | bytes 6488064 | tf_op jit(solution)/shard_map/reduce_scatter | solution.py:195
  583.3 397.6 %reduce-scatter.20.cloned.1.call-start = ((), (), s32[]{:S(2)}) async-start(), calls=%async_computation.24 | async-start | bytes 6488064 | tf_op jit(solution)/shard_map/reduce_scatter | solution.py:198
  594.3 541.7 %reduce-scatter.14.cloned.1.call-start = ((), (), s32[]{:S(2)}) async-start(), calls=%async_computation.21 | async-start | bytes 10813440 | tf_op jit(solution)/shard_map/reduce_scatter | solution.py:375
  659.4 18.0 %all-to-all-start.2 = ((bf16[256,4,512]{0,2,1:T(8,128)(2,1)}), bf16[256,4,512]{0,2,1:T(8,128)(2,1)S(1)}, u32[]{:S(2)}, u32[]{:S(2)}) async-start(bf16[256,4,512]{0,2,1:T(8,128)(2,1)} %bitcast.46), calls=%async_computation.4 | async-start | bytes 2097152 | tf_op jit(solution)/shard_map/all_to_all | solution.py:320
  679.6 58.9 %copy-start.5 = (bf16[1024,2,384]{2,1,0:T(2,128)(2,1)S(1)}, bf16[1024,2,384]{2,1,0:T(2,128)(2,1)}, u32[]{:S(2)}) copy-start(bf16[1024,2,384]{2,1,0:T(2,128)(2,1)} %copy-done.4) | copy-start | bytes 4718596
  811.9 24.6 %all-to-all-start.3 = ((bf16[4,256,768]{2,1,0:T(8,128)(2,1)}), bf16[4,256,768]{2,1,0:T(8,128)(2,1)}, u32[]{:S(2)}, u32[]{:S(2)}) async-start(bf16[4,256,768]{2,1,0:T(8,128)(2,1)} %all_to_all.69), calls=%async_computation.5 | async-start | bytes 3145728 | tf_op jit(solution)/shard_map/all_to_all | solution.py:336
  816.4 491.9 %reduce-scatter.12.cloned.1.call-start = ((), (), s32[]{:S(2)}) async-start(), calls=%async_computation.20 | async-start | bytes 16220160 | tf_op jit(solution)/shard_map/reduce_scatter | solution.py:374
  985.0 151.0 %copy-start.46 = (f32[40,2048]{1,0:T(8,128)S(1)}, f32[40,2048]{1,0:T(8,128)}, u32[]{:S(2)}) copy-start(f32[40,2048]{1,0:T(8,128)} %param.51) | copy-start | bytes 983044
  985.0 151.0 %copy-start.58 = (f32[40,2048]{1,0:T(8,128)S(1)}, f32[40,2048]{1,0:T(8,128)}, u32[]{:S(2)}) copy-start(f32[40,2048]{1,0:T(8,128)} %param.57) | copy-start | bytes 983044
  985.0 151.0 %copy-start.59 = (f32[40,2048]{1,0:T(8,128)S(1)}, f32[40,2048]{1,0:T(8,128)}, u32[]{:S(2)}) copy-start(f32[40,2048]{1,0:T(8,128)} %param.63) | copy-start | bytes 983044
  986.7 321.5 %copy-start.42 = (f32[64,1920]{1,0:T(8,128)S(1)}, f32[64,1920]{1,0:T(8,128)}, u32[]{:S(2)}) copy-start(f32[64,1920]{1,0:T(8,128)} %param.50) | copy-start | bytes 1474564
  986.8 321.5 %copy-start.53 = (f32[64,1920]{1,0:T(8,128)S(1)}, f32[64,1920]{1,0:T(8,128)}, u32[]{:S(2)}) copy-start(f32[64,1920]{1,0:T(8,128)} %param.56) | copy-start | bytes 1474564
  986.8 321.5 %copy-start.54 = (f32[64,1920]{1,0:T(8,128)S(1)}, f32[64,1920]{1,0:T(8,128)}, u32[]{:S(2)}) copy-start(f32[64,1920]{1,0:T(8,128)} %param.62) | copy-start | bytes 1474564
  (97 other events, 1049.2 us)
Sparse Core Ops, SparseCore 0:
  11.5 78.3 all-gather.7
  93.4 67.2 all-gather.9
  163.4 91.4 all-gather.13
  256.9 32.6 all-gather.11
  292.2 92.6 all-gather.15
  386.9 32.6 all-gather.19
  422.4 92.6 all-gather.17
  549.9 42.7 reduce-scatter.9
  595.3 44.4 reduce-scatter.7
  643.3 109.9 reduce-scatter.15
  756.9 109.7 reduce-scatter.17
  870.2 110.5 reduce-scatter.19
  983.1 152.7 reduce-scatter.13
  1141.8 166.3 reduce-scatter.11
where the time goes:
time: 1330 us; the launch traced here: 1320 us
  waiting for transfers between devices  733 us (55%)
  matrix products  235 us (18%)
  local copies, waits for them, and re-layouts  104 us (8%)
  blocking collectives  102 us (8%)
  other arithmetic  100 us (8%)
  between operations  16.9 us (1%)
  loops' own time  14.6 us (1%)
  starting transfers between devices  13.3 us (1%)
    reduce_scatter x1, waiting for transfers between devices, local(): lax.psum_scatter(grad_mixer, ('seq', 'kv'), scatter_dimension=0, tiled=True)  169 us
    reduce_scatter x1, waiting for transfers between devices, local(): lax.psum_scatter(grad_output, ('seq', 'kv'), scatter_dimension=0, tiled=T...  149 us
    all_gather x1, waiting for transfers between devices, local(): lax.all_gather(down_weight.astype(jnp.bfloat16), 'seq', axis=0, tiled=True)  95.4 us
    unnamed x2, blocking collectives  84.6 us
    all_gather x1, waiting for transfers between devices, local(): lax.all_gather(up_weight.astype(jnp.bfloat16), 'seq', axis=0, tiled=True)  83.6 us
    dot_general x5, matrix products, contract_rows(): lax.dot_general(left, right, (((0,), (0,)), ((), ())), preferred_element_...  47.5 us
    reduce_scatter x1, waiting for transfers between devices, local(): lax.psum_scatter(partial_out.astype(jnp.bfloat16), 'kv', scatter_dimensio...  42.7 us
    dot_general x5, matrix products, contract_cols(): lax.dot_general(left, right, (((1,), (1,)), ((), ())), preferred_element_...  41.9 us
  transfers between devices with their start and end apart: 17, of which 13 were waited for; matrix products, arithmetic and copies ran while one was open for 29% of the time, Pallas kernels for 0%

commit v1 on v0

v1 whole, which is shorter than its diff:
```python
import functools

import jax
import jax.numpy as jnp
import numpy as np
from jax import lax
from jax.experimental import pallas as pl
from jax.experimental.pallas import tpu as pltpu
from jax.sharding import Mesh, PartitionSpec as P

QUERY_HEADS = 20
VALUE_GROUPS = 5
HEAD_SIZE = 64

eps_norm = 1e-06
masked_value = -1e30
beta_first = 0.9
beta_second = 0.95
adam_eps = 1e-08

ALL = ("sh", "sl", "kh", "kl")
SEQ = ("sh", "sl")
KV = ("kh", "kl")
OWNERS = ("sh", "kl")
VMEM_LIMIT = 40 * 1024 * 1024


def rms_scale(value_rows):
    return lax.rsqrt(jnp.mean(value_rows * value_rows, -1, keepdims=True) + eps_norm)


def norm_back(grad_out, value_rows, scale, gain):
    shaped = value_rows * scale
    pushed = grad_out * gain
    grad_in = scale * (pushed - shaped * jnp.mean(pushed * shaped, -1, keepdims=True))
    return (grad_in, grad_out * shaped)


def angle_tables(item_count):
    places = np.arange(item_count).astype(np.float32)
    steps = np.arange(HEAD_SIZE // 2).astype(np.float32) * np.float32(2.0) / np.float32(HEAD_SIZE)
    freqs = np.float32(10000.0) ** (-steps)
    angles = freqs[:, None].astype(np.float32) * places[None, :]
    return (np.cos(angles).astype(np.float32), np.sin(angles).astype(np.float32))


def contract(left, right, left_dim, right_dim):
    return lax.dot_general(
        left,
        right,
        (((left_dim,), (right_dim,)), ((), ())),
        preferred_element_type=jnp.float32,
    )


def head_scale(rows):
    return lax.rsqrt(jnp.mean(rows * rows, 0, keepdims=True) + eps_norm)


def rotated(rows, scale, gain, cosine, sine):
    half = HEAD_SIZE // 2
    shaped = rows * scale * gain
    first, second = shaped[:half], shaped[half:]
    return jnp.concatenate(
        [first * cosine - second * sine, second * cosine + first * sine], axis=0
    )


def unrotated_norm_back(grad, rows, scale, gain, cosine, sine):
    half = HEAD_SIZE // 2
    first, second = grad[:half], grad[half:]
    turned = jnp.concatenate(
        [first * cosine + second * sine, second * cosine - first * sine], axis=0
    )
    shaped = rows * scale
    pushed = turned * gain
    grad_in = scale * (pushed - shaped * jnp.mean(pushed * shaped, 0, keepdims=True))
    return (grad_in, turned * shaped)


def causal(block):
    keys = lax.broadcasted_iota(jnp.int32, (block, block), 0)
    places = lax.broadcasted_iota(jnp.int32, (block, block), 1)
    return keys <= places


def forward_kernel(
    group_ref, qp_ref, kp_ref, vp_ref, cos_ref, sin_ref, gq_ref, gk_ref,
    q_ref, k_ref, v_ref, out_ref, lse_ref, *, block,
):
    cosine, sine = cos_ref[...], sin_ref[...]
    qp, kp = qp_ref[...], kp_ref[...]
    query = (rotated(qp, head_scale(qp), gq_ref[...], cosine, sine) * 0.125).astype(jnp.bfloat16)
    key = rotated(kp, head_scale(kp), gk_ref[...], cosine, sine).astype(jnp.bfloat16)
    value = vp_ref[...].astype(jnp.bfloat16)
    q_ref[0] = query
    k_ref[0] = key
    v_ref[0] = value
    allowed = causal(block)
    for index in range(query.shape[1] // block):
        start, stop = index * block, (index + 1) * block
        part = query[:, start:stop]
        near = contract(key[:, start:stop], part, 0, 0)
        near = jnp.where(allowed, near, masked_value)
        top = jnp.max(near, 0, keepdims=True)
        if index:
            far = contract(key[:, :start], part, 0, 0)
            top = jnp.maximum(top, jnp.max(far, 0, keepdims=True))
        near = jnp.exp(near - top)
        total = jnp.sum(near, 0, keepdims=True)
        if index:
            far = jnp.exp(far - top)
            total = total + jnp.sum(far, 0, keepdims=True)
        share = 1.0 / total
        result = contract(value[:, start:stop], (near * share).astype(jnp.bfloat16), 1, 0)
        if index:
            result = result + contract(value[:, :start], (far * share).astype(jnp.bfloat16), 1, 0)
        out_ref[0, :, start:stop] = result.astype(jnp.bfloat16)
        lse_ref[0, :, start:stop] = top + jnp.log(total)


def backward_kernel(
    group_ref, qp_ref, kp_ref, q_ref, k_ref, v_ref, do_ref, lse_ref, cos_ref, sin_ref,
    gq_ref, gk_ref,
    gqp_ref, gkp_ref, gv_ref, gain_q_ref, gain_k_ref,
    dq_ref, dk_ref, dv_ref, sum_q_ref, sum_k_ref, *, block,
):
    head = pl.program_id(0)
    heads = pl.num_programs(0)
    group = group_ref[head]
    opens = jnp.logical_or(head == 0, group_ref[jnp.maximum(head - 1, 0)] != group)
    closes = jnp.logical_or(
        head == heads - 1, group_ref[jnp.minimum(head + 1, heads - 1)] != group
    )

    @pl.when(head == 0)
    def _():
        sum_q_ref[...] = jnp.zeros_like(sum_q_ref)
        sum_k_ref[...] = jnp.zeros_like(sum_k_ref)

    @pl.when(opens)
    def _():
        dk_ref[...] = jnp.zeros_like(dk_ref)
        dv_ref[...] = jnp.zeros_like(dv_ref)

    query, key, value, grad = q_ref[0], k_ref[0], v_ref[0], do_ref[...]
    allowed = causal(block)
    for index in range(query.shape[1] // block):
        start, stop = index * block, (index + 1) * block
        part, grad_part = query[:, start:stop], grad[:, start:stop]
        sums_log = lse_ref[0, :, start:stop]
        near = jnp.exp(contract(key[:, start:stop], part, 0, 0) - sums_log)
        near = jnp.where(allowed, near, 0.0)
        grad_near = contract(value[:, start:stop], grad_part, 0, 0)
        inner = jnp.sum(near * grad_near, 0, keepdims=True)
        if index:
            far = jnp.exp(contract(key[:, :start], part, 0, 0) - sums_log)
            grad_far = contract(value[:, :start], grad_part, 0, 0)
            inner = inner + jnp.sum(far * grad_far, 0, keepdims=True)
        step = (near * (grad_near - inner)).astype(jnp.bfloat16)
        total = contract(key[:, start:stop], step, 1, 0)
        dk_ref[:, start:stop] += contract(part, step, 1, 1)
        dv_ref[:, start:stop] += contract(grad_part, near.astype(jnp.bfloat16), 1, 1)
        if index:
            step = (far * (grad_far - inner)).astype(jnp.bfloat16)
            total = total + contract(key[:, :start], step, 1, 0)
            dk_ref[:, :start] += contract(part, step, 1, 1)
            dv_ref[:, :start] += contract(grad_part, far.astype(jnp.bfloat16), 1, 1)
        dq_ref[:, start:stop] = total * 0.125

    cosine, sine = cos_ref[...], sin_ref[...]
    qp = qp_ref[...]
    grad_qp, gain_terms = unrotated_norm_back(
        dq_ref[...].astype(jnp.bfloat16).astype(jnp.float32),
        qp, head_scale(qp), gq_ref[...], cosine, sine,
    )
    gqp_ref[...] = grad_qp.astype(jnp.bfloat16)
    sum_q_ref[...] += gain_terms

    @pl.when(closes)
    def _():
        kp = kp_ref[...]
        grad_kp, terms = unrotated_norm_back(
            dk_ref[...].astype(jnp.bfloat16).astype(jnp.float32),
            kp, head_scale(kp), gk_ref[...], cosine, sine,
        )
        gkp_ref[0] = grad_kp.astype(jnp.bfloat16)
        gv_ref[0] = dv_ref[...].astype(jnp.bfloat16)
        sum_k_ref[...] += terms

    @pl.when(head == heads - 1)
    def _():
        gain_q_ref[...] = jnp.sum(sum_q_ref[...], 1, keepdims=True)
        gain_k_ref[...] = jnp.sum(sum_k_ref[...], 1, keepdims=True)


def attention_specs(length, heads):
    half = HEAD_SIZE // 2
    tall = (HEAD_SIZE, length)
    whole = lambda shape: pl.BlockSpec(shape, lambda h, g: (0, 0))
    per_head = pl.BlockSpec((1,) + tall, lambda h, g: (h, 0, 0))
    per_group = pl.BlockSpec((1,) + tall, lambda h, g: (g[h], 0, 0))
    per_row = pl.BlockSpec((1, 1, length), lambda h, g: (h, 0, 0))
    query = pl.BlockSpec(tall, lambda h, g: (h, 0))
    key = pl.BlockSpec(tall, lambda h, g: (heads + g[h], 0))
    value = pl.BlockSpec(tall, lambda h, g: (heads + 2 + g[h], 0))
    table = whole((half, length))
    gain = whole((HEAD_SIZE, 1))
    return (query, key, value, per_head, per_group, per_row, table, gain)


def attend(groups, mixed, cosine, sine, gain_q, gain_k, heads):
    length = mixed.shape[1]
    query, key, value, per_head, per_group, per_row, table, gain = attention_specs(length, heads)
    per = lambda count: jax.ShapeDtypeStruct((count, HEAD_SIZE, length), jnp.bfloat16)
    scores = heads * length * length // 2
    return pl.pallas_call(
        functools.partial(forward_kernel, block=min(256, length)),
        name="attention_forward",
        out_shape=(
            per(heads), per(2), per(2), per(heads),
            jax.ShapeDtypeStruct((heads, 1, length), jnp.float32),
        ),
        grid_spec=pltpu.PrefetchScalarGridSpec(
            num_scalar_prefetch=1,
            grid=(heads,),
            in_specs=[query, key, value, table, table, gain, gain],
            out_specs=[per_head, per_group, per_group, per_head, per_row],
        ),
        compiler_params=pltpu.CompilerParams(
            dimension_semantics=("arbitrary",), vmem_limit_bytes=VMEM_LIMIT
        ),
        cost_estimate=pl.CostEstimate(
            flops=scores * 4 * HEAD_SIZE, transcendentals=scores, bytes_accessed=8_000_000
        ),
    )(groups, mixed, mixed, mixed, cosine, sine, gain_q, gain_k)


def attend_back(groups, mixed, query_rows, key_rows, value_rows, grads, lse, cosine, sine, gain_q, gain_k, heads):
    length = mixed.shape[1]
    query, key, value, per_head, per_group, per_row, table, gain = attention_specs(length, heads)
    tall = (HEAD_SIZE, length)
    scores = heads * length * length // 2
    return pl.pallas_call(
        functools.partial(backward_kernel, block=min(256, length)),
        name="attention_backward",
        out_shape=(
            jax.ShapeDtypeStruct((heads * HEAD_SIZE, length), jnp.bfloat16),
            jax.ShapeDtypeStruct((2,) + tall, jnp.bfloat16),
            jax.ShapeDtypeStruct((2,) + tall, jnp.bfloat16),
            jax.ShapeDtypeStruct((HEAD_SIZE, 1), jnp.float32),
            jax.ShapeDtypeStruct((HEAD_SIZE, 1), jnp.float32),
        ),
        grid_spec=pltpu.PrefetchScalarGridSpec(
            num_scalar_prefetch=1,
            grid=(heads,),
            in_specs=[
                query, key, per_head, per_group, per_group, query, per_row, table, table, gain, gain,
            ],
            out_specs=[query, per_group, per_group, gain, gain],
            scratch_shapes=[pltpu.VMEM(tall, jnp.float32)] * 5,
        ),
        compiler_params=pltpu.CompilerParams(
            dimension_semantics=("arbitrary",), vmem_limit_bytes=VMEM_LIMIT
        ),
        cost_estimate=pl.CostEstimate(
            flops=scores * 10 * HEAD_SIZE, transcendentals=scores, bytes_accessed=10_000_000
        ),
    )(groups, mixed, mixed, query_rows, key_rows, value_rows, grads, lse, cosine, sine, gain_q, gain_k)


def adamw(weight, grad, first, second, rate, shrink, item_count):
    first_new = beta_first * first + (1.0 - beta_first) * grad
    second_new = beta_second * second + (1.0 - beta_second) * grad * grad
    fix_first = 1.0 - jnp.power(beta_first, item_count)
    fix_second = 1.0 - jnp.power(beta_second, item_count)
    stepped = first_new / fix_first / (jnp.sqrt(second_new / fix_second) + adam_eps)
    return (
        weight - rate * (stepped + shrink * weight),
        jnp.stack([first_new, jnp.sqrt(second_new)]),
    )


def local(
    sizes,
    tokens,
    cotangent,
    corpus_id,
    corpus_weight,
    step_count,
    qkv_weight,
    out_weight,
    gains,
    gate_weight,
    up_weight,
    down_weight,
    first_qkv,
    first_out,
    first_gains,
    first_gate,
    first_up,
    first_down,
    second_qkv,
    second_out,
    second_gains,
    second_gate,
    second_up,
    second_down,
):
    low = jnp.bfloat16
    high = jnp.float32
    devices = int(np.prod(sizes))
    seqs = sizes[0] * sizes[1]
    parts = sizes[2] * sizes[3]
    places = np.arange(devices).reshape(sizes)
    where = np.stack(np.unravel_index(np.arange(devices), sizes), -1)

    def permute(array, target):
        pairs = [(int(i), int(places[tuple(target(*where[i]))])) for i in range(devices)]
        return lax.ppermute(array, ALL, pairs)

    def swap(array):
        return permute(array, lambda sh, sl, kh, kl: (sh, kl, kh, sl))

    def in_ffn_group(array, r):
        return permute(array, lambda sh, sl, kh, kl: (sh, sl ^ (r & 1), kh ^ (r >> 1), kl))

    def in_sequence(array, r):
        return permute(array, lambda sh, sl, kh, kl: (sh, sl, kh ^ (r >> 1), kl ^ (r & 1)))

    item_count, model = tokens.shape
    heads = QUERY_HEADS // parts
    width = heads * HEAD_SIZE
    pair = 2 * HEAD_SIZE
    keys_at = QUERY_HEADS * HEAD_SIZE
    values_at = keys_at + VALUE_GROUPS * HEAD_SIZE
    kv = lax.axis_index(KV)
    length = item_count * parts
    cosine, sine = angle_tables(length)
    groups = ((jnp.arange(heads, dtype=jnp.int32) + kv) // 4).astype(jnp.int32)

    qkv_low = qkv_weight.astype(low)
    qkv_parts = jnp.stack(
        [
            jnp.concatenate(
                [
                    qkv_low[:, d * width : (d + 1) * width],
                    qkv_low[:, keys_at + d * HEAD_SIZE : keys_at + d * HEAD_SIZE + pair],
                    qkv_low[:, values_at + d * HEAD_SIZE : values_at + d * HEAD_SIZE + pair],
                ],
                axis=1,
            )
            for d in range(parts)
        ]
    )
    qkv_rows = lax.all_to_all(qkv_parts, KV, split_axis=0, concat_axis=0, tiled=True)
    qkv_full = lax.all_gather(
        qkv_rows.reshape(-1, width + 2 * pair), SEQ, axis=0, tiled=True
    )
    gains_low = lax.all_to_all(
        jnp.broadcast_to(gains.astype(low)[None], (devices, gains.shape[0])),
        ALL, split_axis=0, concat_axis=0, tiled=True,
    ).reshape(-1)
    gain_values = gains_low.astype(high)
    out_rows = lax.all_gather(out_weight.astype(low), SEQ, axis=0, tiled=True)
    gate_full = lax.all_gather(swap(gate_weight.astype(low)), OWNERS, axis=0, tiled=True)
    up_full = lax.all_gather(swap(up_weight.astype(low)), OWNERS, axis=0, tiled=True)
    down_full = lax.all_gather(swap(down_weight.astype(low)), OWNERS, axis=0, tiled=True)

    all_rows = jnp.zeros((parts, item_count, model), low)
    all_rows = lax.dynamic_update_slice_in_dim(all_rows, tokens[None], kv, 0)
    for r in range(1, parts):
        all_rows = lax.dynamic_update_slice_in_dim(
            all_rows, in_sequence(tokens, r)[None], kv ^ r, 0
        )
    all_rows = all_rows.reshape(length, model).astype(high)
    normed = (all_rows * rms_scale(all_rows) * gain_values[:model]).astype(low)

    factor = jnp.sum(
        jnp.where(jnp.arange(corpus_weight.shape[0]) == corpus_id[0], corpus_weight, 0.0)
    )
    weighted = cotangent.astype(high) * factor
    weighted_low = weighted.astype(low)
    weighted_rows = jnp.concatenate(
        [weighted_low] + [in_ffn_group(weighted_low, r) for r in range(1, 4)], axis=0
    )

    gain_q = gain_values[2 * model : 2 * model + HEAD_SIZE].reshape(HEAD_SIZE, 1)
    gain_k = gain_values[2 * model + HEAD_SIZE :].reshape(HEAD_SIZE, 1)
    mixed = contract(qkv_full, normed, 0, 1)
    query_rows, key_rows, value_rows, result, lse = attend(
        groups, mixed, cosine, sine, gain_q, gain_k, heads
    )
    outgoing = jnp.stack(
        [result.reshape(width, length)[:, d * item_count : (d + 1) * item_count] for d in range(parts)]
    )
    attended = lax.all_to_all(outgoing, KV, split_axis=0, concat_axis=0, tiled=True).reshape(
        parts * width, item_count
    )

    out_near = out_rows.reshape(seqs, 1, -1, model)
    out_far = in_sequence(out_near, 2)
    out_full = jnp.zeros((seqs, parts) + out_near.shape[2:], low)
    for r, piece in enumerate((out_near, in_sequence(out_near, 1), out_far, in_sequence(out_far, 1))):
        out_full = lax.dynamic_update_slice_in_dim(out_full, piece, kv ^ r, 1)
    out_full = out_full.reshape(-1, model)
    inputs = tokens.astype(high)
    hidden = inputs + contract(attended, out_full, 0, 0)

    scale_two = rms_scale(hidden)
    gain_two = gain_values[model : 2 * model]
    normed_two = (hidden * scale_two * gain_two).astype(low)
    ffn_rows = jnp.concatenate(
        [normed_two] + [in_ffn_group(normed_two, r) for r in range(1, 4)], axis=0
    )
    gate = contract(ffn_rows, gate_full, 1, 0)
    up_part = contract(ffn_rows, up_full, 1, 0)
    sigma = jax.nn.sigmoid(gate)
    swish = gate * sigma
    acted = (swish * up_part).astype(low)

    def to_owners(partial):
        blocks = partial.reshape(4, item_count, model)
        total = blocks[0]
        for r in range(1, 4):
            total = total + in_ffn_group(blocks[r].astype(low), r).astype(high)
        return total

    def share(grad):
        return swap(
            lax.psum_scatter(grad.astype(low), OWNERS, scatter_dimension=0, tiled=True)
        ).astype(high)

    grad_down = share(contract(weighted_rows, acted, 0, 0))
    grad_acted = contract(weighted_rows, down_full, 1, 0)
    grad_gate = (grad_acted * up_part * sigma * (1.0 + gate * (1.0 - sigma))).astype(low)
    grad_up = (grad_acted * swish).astype(low)
    grad_normed_two = to_owners(
        contract(grad_gate, gate_full, 1, 1) + contract(grad_up, up_full, 1, 1)
    )
    grad_gate_w = share(contract(ffn_rows, grad_gate, 0, 0))
    grad_up_w = share(contract(ffn_rows, grad_up, 0, 0))
    ffn = to_owners(contract(acted, down_full, 1, 1))
    block_out = (hidden + ffn).astype(low)

    pushed_two, gain_two_terms = norm_back(grad_normed_two, hidden, scale_two, gain_two)
    grad_hidden = weighted + pushed_two
    hidden_low = grad_hidden.astype(low)

    attended_gradient = contract(out_full, hidden_low, 1, 1).astype(low)
    incoming = lax.all_to_all(
        attended_gradient.reshape(parts, width, item_count), KV, split_axis=0, concat_axis=0, tiled=True
    )
    grads = jnp.concatenate([incoming[d] for d in range(parts)], axis=1)
    grad_queries, grad_keys, grad_values, gain_q_sum, gain_k_sum = attend_back(
        groups, mixed, query_rows, key_rows, value_rows, grads, lse,
        cosine, sine, gain_q, gain_k, heads,
    )
    grad_mixed = jnp.concatenate(
        [grad_queries, grad_keys.reshape(pair, length), grad_values.reshape(pair, length)], axis=0
    )
    grad_mixer = contract(normed, grad_mixed, 0, 1).astype(low)
    mixer_share = lax.psum_scatter(grad_mixer, SEQ, scatter_dimension=0, tiled=True)
    mixer_parts = lax.all_to_all(
        mixer_share.reshape(parts, -1, width + 2 * pair), KV, split_axis=0, concat_axis=0, tiled=True
    ).astype(high)
    slots = [[None] * VALUE_GROUPS, [None] * VALUE_GROUPS]
    for d in range(parts):
        for kind in range(2):
            for j in range(2):
                at = width + kind * pair + j * HEAD_SIZE
                piece = mixer_parts[d, :, at : at + HEAD_SIZE]
                held = slots[kind][d + j]
                slots[kind][d + j] = piece if held is None else held + piece
    qkv_grad = jnp.concatenate(
        [mixer_parts[d, :, :width] for d in range(parts)] + slots[0] + slots[1], axis=1
    )

    grad_normed = contract(grad_mixed, qkv_full, 0, 1).astype(low)
    grad_normed = jnp.sum(
        lax.all_to_all(
            grad_normed.reshape(parts, item_count, model), KV, split_axis=0, concat_axis=0, tiled=True
        ).astype(high),
        axis=0,
    )
    pushed_one, gain_one_terms = norm_back(
        grad_normed, inputs, rms_scale(inputs), gain_values[:model]
    )
    grad_input = grad_hidden + pushed_one

    grad_output = contract(attended, hidden_low, 1, 0)
    blocks = grad_output.reshape(seqs, 2, 2, -1, model)
    is_low = lax.axis_index("kl") == 0
    kept = jnp.where(is_low, blocks[:, :, 0], blocks[:, :, 1])
    sent = jnp.where(is_low, blocks[:, :, 1], blocks[:, :, 0]).astype(low)
    blocks = kept + in_sequence(sent, 1).astype(high)
    is_first = lax.axis_index("kh") == 0
    kept = jnp.where(is_first, blocks[:, 0], blocks[:, 1])
    sent = jnp.where(is_first, blocks[:, 1], blocks[:, 0]).astype(low)
    blocks = kept + in_sequence(sent, 2).astype(high)
    out_grad = lax.psum_scatter(
        blocks.astype(low).reshape(-1, model), SEQ, scatter_dimension=0, tiled=True
    ).astype(high)

    grad_gains = jnp.concatenate(
        [
            jnp.sum(gain_one_terms, 0),
            jnp.sum(gain_two_terms, 0),
            gain_q_sum.reshape(-1),
            gain_k_sum.reshape(-1),
        ]
    )
    gains_grad = jnp.sum(
        lax.all_to_all(
            grad_gains.reshape(devices, -1), ALL, split_axis=0, concat_axis=0, tiled=True
        ),
        axis=0,
    )

    steps_done = step_count[0].astype(high)
    new_qkv, moments_qkv = adamw(qkv_weight, qkv_grad, first_qkv, second_qkv, 0.02, 0.1, steps_done)
    new_out, moments_out = adamw(out_weight, out_grad, first_out, second_out, 0.2, 0.1, steps_done)
    new_gains, moments_gains = adamw(
        gains, gains_grad, first_gains, second_gains, 0.6, 0.0, steps_done
    )
    new_gate, moments_gate = adamw(
        gate_weight, grad_gate_w, first_gate, second_gate, 0.02, 0.1, steps_done
    )
    new_up, moments_up = adamw(up_weight, grad_up_w, first_up, second_up, 0.02, 0.1, steps_done)
    new_down, moments_down = adamw(
        down_weight, grad_down, first_down, second_down, 0.013, 0.1, steps_done
    )
    return (
        block_out,
        grad_input,
        new_qkv,
        moments_qkv,
        new_out,
        moments_out,
        new_gains,
        moments_gains,
        new_gate,
        moments_gate,
        new_up,
        moments_up,
        new_down,
        moments_down,
    )


def solution(mesh):
    seqs, parts = mesh.shape["seq"], mesh.shape["kv"]
    sizes = (seqs // 2, 2, parts // 2, 2)
    fine = Mesh(mesh.devices.reshape(sizes), ALL)
    rows = P(ALL, None)
    block = P(SEQ, KV)
    return jax.shard_map(
        functools.partial(local, sizes),
        mesh=fine,
        in_specs=(
            rows, rows, P(SEQ), P(), P(),
            rows, rows, P(ALL), block, block, block,
            rows, rows, P(ALL), block, block, block,
            rows, rows, P(ALL), block, block, block,
        ),
        out_specs=(
            rows, rows,
            rows, P(None, ALL, None),
            rows, P(None, ALL, None),
            P(ALL), P(None, ALL),
            block, P(None, SEQ, KV),
            block, P(None, SEQ, KV),
            block, P(None, SEQ, KV),
        ),
        check_vma=False,
    )
```

time: 1330 us -> 848 us (0.64)
  waiting for transfers between devices: 733 us -> 433 us
  matrix products: 235 us -> 139 us
  blocking collectives: 102 us -> 23.9 us
  starting transfers between devices: 13.3 us -> 89 us
  local copies, waits for them, and re-layouts: 104 us -> 41.3 us
  other arithmetic: 100 us -> 68 us
  Pallas kernels: 0 us -> 25.3 us
  loops' own time: 14.6 us -> 0 us
    all_gather x7 -> x5, waiting for transfers between devices: 293 us -> 17.7 us  [the longest x1 17.7 us: local(): lax.all_gather(swap(gate_weight.astype(low)), OWNERS, axis=0, tiled=True)]
    reduce_scatter x7 -> x5, waiting for transfers between devices: 385 us -> 135 us  [the longest x3 121 us: share(): lax.psum_scatter(grad.astype(low), OWNERS, scatter_dimension=0, tiled=True)]
    ppermute x0 -> x26, waiting for transfers between devices: none -> 188 us  [permute(): return lax.ppermute(array, ALL, pairs)]
    dot_general x43 -> x15, matrix products: 235 us -> 139 us  [contract(): lax.dot_general(left, right, (((left_dim,), (right_dim,)), ((), ())), pre...]
    unnamed x2 -> x0, blocking collectives: 84.6 us -> none
    ppermute x0 -> x26, starting transfers between devices: none -> 68.1 us  [permute(): return lax.ppermute(array, ALL, pairs)]
    all_to_all x3 -> x5, waiting for transfers between devices: 54.5 us -> 91.6 us  [the longest x1 46.9 us: local(): lax.all_to_all(grad_normed.reshape(parts, item_count, model), KV, split_a...]
    pallas_call x0 -> x2, Pallas kernels: none -> 25.3 us  [the longest x1 14.9 us: attend_back(): pl.pallas_call(functools.partial(backward_kernel, block=min(256, length))...]
  transfers between devices with their start and end apart: 17 -> 41, of which waited for: 13 -> 19; matrix products, arithmetic and copies ran while one was open for 29% -> 20% of each run, Pallas kernels for 0% -> 1%
where the time goes in v1:
time: 848 us; the launch traced here: 836 us
  waiting for transfers between devices  433 us (51%)
  matrix products  139 us (16%)
  starting transfers between devices  89 us (10%)
  other arithmetic  68 us (8%)
  local copies, waits for them, and re-layouts  41.3 us (5%)
  Pallas kernels  25.3 us (3%)
  blocking collectives  23.9 us (3%)
  between operations  16.9 us (2%)
    ppermute x26, waiting for transfers between devices, permute(): return lax.ppermute(array, ALL, pairs)  188 us
    dot_general x15, matrix products, contract(): lax.dot_general(left, right, (((left_dim,), (right_dim,)), ((), ())), pre...  139 us
    reduce_scatter x3, waiting for transfers between devices, share(): lax.psum_scatter(grad.astype(low), OWNERS, scatter_dimension=0, tiled=True)  121 us
    ppermute x26, starting transfers between devices, permute(): return lax.ppermute(array, ALL, pairs)  68.1 us
    all_to_all x1, waiting for transfers between devices, local(): lax.all_to_all(grad_normed.reshape(parts, item_count, model), KV, split_a...  46.9 us
    all_to_all x1, waiting for transfers between devices, local(): lax.all_to_all(jnp.broadcast_to(gains.astype(low)[None], (devices, gains....  30.3 us
    another operation x11, other arithmetic, adamw(): jnp.stack([first_new, jnp.sqrt(second_new)])  21.8 us
    all_gather x1, waiting for transfers between devices, local(): lax.all_gather(swap(gate_weight.astype(low)), OWNERS, axis=0, tiled=True)  17.7 us
  transfers between devices with their start and end apart: 41, of which 19 were waited for; matrix products, arithmetic and copies ran while one was open for 20% of the time, Pallas kernels for 1%

profile of v1, /device:TPU:0, one launch (start us, length us, event | category | flops | bytes accessed | tf_op | source)
XLA Modules:
  0.0 836.4 jit_solution(1957879651397469166)
XLA Ops:
  10.6 10.9 %all_to_all.40 = bf16[4,64,576]{2,1,0:T(8,128)(2,1)} all-to-all(bf16[4,64,576]{2,1,0:T(8,128)(2,1)S(1)} %pad_maximum_fusion.14), channel_id=1, replica_groups=mesh['sh'=4,'sl'=2,'kh'=2,'kl'=2] {'kh','kl'}, dimensions={0} | all-to-all | bytes 589824 | tf_op jit(solution)/shard_map/all_to_all | solution.py:356
  26.7 30.0 %collective-permute-start = (bf16[256,2048]{1,0:T(8,128)(2,1)S(1)}, bf16[256,2048]{1,0:T(8,128)(2,1)}, u32[]{:S(2)}, u32[]{:S(2)}) collective-permute-start(bf16[256,2048]{1,0:T(8,128)(2,1)S(1)} %copy-done.15), channel_id=1, source_target_pairs={{0,1},{1,0},{2,3},{3,2},{4,5},{5,4},{6,7},{7,6},{8,9},{9,8},{10,11... | collective-permute-start | bytes 3145736 | tf_op jit(solution)/shard_map/ppermute | solution.py:320
  75.1 30.3 %all-to-all-done.1 = bf16[32,1,132]{2,1,0:T(2,128)(2,1)S(1)} async-done(((bf16[32,1,132]{2,1,0:T(2,128)(2,1)}), bf16[32,1,132]{2,1,0:T(2,128)(2,1)S(1)}, u32[]{:S(2)}, u32[]{:S(2)}) %all-to-all-start.1) | async-done | bytes 8480 | tf_op jit(solution)/shard_map/all_to_all | solution.py:360
  129.7 48.1 %collective-permute-done.4 = bf16[8,1,40,2048]{3,2,1,0:T(8,128)(2,1)} collective-permute-done((bf16[8,1,40,2048]{3,2,1,0:T(8,128)(2,1)}, bf16[8,1,40,2048]{3,2,1,0:T(8,128)(2,1)}, u32[]{:S(2)}, u32[]{:S(2)}) %collective-permute-start.4) | collective-permute-done | bytes 1310752 | tf_op jit(solution)/shard_map/ppermute | solution.py:320
  222.0 13.0 %fusion.37 = f32[1024,1408]{1,0:T(8,128)} fusion(bf16[2048,1408]{1,0:T(8,128)(2,1)} %all-gather.14.cloned.1.call-done, bf16[256,2048]{1,0:T(8,128)(2,1)} %collective-permute-done.17, bf16[256,2048]{1,0:T(8,128)(2,1)} %collective-permute-done.16, bf16[256,2048]{1,0:T(8,128)(2,1)} %collective-permute-done.15, bf16[256,2048]{1,0:T(8,128)(2,1)} %fusion.24), kind=kOutput, calls=%fused_computation.90 | convolution fusion | flops 5922357248 | bytes 15728640 | tf_op jit(solution)/shard_map/dot_general | solution.py:48
  245.9 20.2 %collective-permute-done.7 = bf16[256,2048]{1,0:T(8,128)(2,1)} collective-permute-done((bf16[256,2048]{1,0:T(8,128)(2,1)}, bf16[256,2048]{1,0:T(8,128)(2,1)}, u32[]{:S(2)}, u32[]{:S(2)}) %collective-permute-start.7) | collective-permute-done | bytes 1048608 | tf_op jit(solution)/shard_map/ppermute | solution.py:320
  266.9 12.7 %fusion.58 = f32[1024,1408]{1,0:T(8,128)} fusion(bf16[2048,1408]{1,0:T(8,128)(2,1)} %all-gather.12.cloned.1.call-done, bf16[256,2048]{1,0:T(8,128)(2,1)} %collective-permute-done.8, bf16[256,2048]{1,0:T(8,128)(2,1)} %collective-permute-done.7, bf16[256,2048]{1,0:T(8,128)(2,1)} %collective-permute-done.6, bf16[256,2048]{1,0:T(8,128)(2,1)} %multiply_convert_fusion.3), kind=kOutput, calls=%fused_computation.169 | convolution fusion | flops 5922357248 | bytes 15728640 | tf_op jit(solution)/shard_map/dot_general | solution.py:48
  279.6 17.7 %all-gather.10.cloned.1.call-done = bf16[2048,1408]{1,0:T(8,128)(2,1)} async-done(((bf16[256,1408]{1,0:T(8,128)(2,1)}), bf16[2048,1408]{1,0:T(8,128)(2,1)}) %all-gather.10.cloned.1.call-update) | async-done | bytes 5767184 | tf_op jit(solution)/shard_map/all_gather | solution.py:366
  297.3 16.5 %multiply_convert_fusion.1 = (bf16[1024,1408]{1,0:T(8,128)(2,1)}, bf16[1024,1408]{1,0:T(8,128)(2,1)S(1)}, bf16[1024,1408]{1,0:T(8,128)(2,1)}) fusion(f32[1024,1408]{1,0:T(8,128)} %fusion.37, f32[1024,1408]{1,0:T(8,128)} %fusion.58, bf16[2048,1408]{1,0:T(8,128)(2,1)} %all-gather.10.cloned.1.call-done, bf16[256,2048]{1,0:T(8,128)(2,1)} %collective-permute-done.8, ...), kind=kOutput, calls=%fused_computation.9 | convolution fusion | flops 5943984128 | bytes 30146560 | tf_op jit(solution)/shard_map/dot_general | solution.py:48
  313.8 11.8 %fusion.69 = f32[1024,2048]{1,0:T(8,128)} fusion(bf16[1024,1408]{1,0:T(8,128)(2,1)S(1)} %get-tuple-element.42, bf16[2048,1408]{1,0:T(8,128)(2,1)} %all-gather.12.cloned.1.call-done), kind=kOutput, calls=%fused_computation.179 | convolution fusion | flops 5905580032 | bytes 17039360 | tf_op jit(solution)/shard_map/dot_general | solution.py:48
  325.7 13.1 %fusion.66 = (bf16[1024,2048]{1,0:T(8,128)(2,1)S(1)}, f32[1024,2048]{1,0:T(8,128)}) fusion(f32[1024,2048]{1,0:T(8,128)} %fusion.69, bf16[1024,1408]{1,0:T(8,128)(2,1)S(1)} %copy-done.48, bf16[2048,1408]{1,0:T(8,128)(2,1)} %all-gather.10.cloned.1.call-done), kind=kOutput, calls=%fused_computation.176 | convolution fusion | flops 5909774336 | bytes 29622272 | tf_op jit(solution)/shard_map/dot_general | solution.py:48
  367.6 21.0 %collective-permute-done.19 = bf16[256,2048]{1,0:T(8,128)(2,1)S(1)} collective-permute-done((bf16[256,2048]{1,0:T(8,128)(2,1)S(1)}, bf16[256,2048]{1,0:T(8,128)(2,1)S(1)}, u32[]{:S(2)}, u32[]{:S(2)}) %collective-permute-start.19) | collective-permute-done | bytes 1048608 | tf_op jit(solution)/shard_map/ppermute | solution.py:320
  391.5 19.6 %collective-permute-done.14 = bf16[256,2048]{1,0:T(8,128)(2,1)S(1)} collective-permute-done((bf16[256,2048]{1,0:T(8,128)(2,1)S(1)}, bf16[256,2048]{1,0:T(8,128)(2,1)S(1)}, u32[]{:S(2)}, u32[]{:S(2)}) %collective-permute-start.14) | collective-permute-done | bytes 1048608 | tf_op jit(solution)/shard_map/ppermute | solution.py:320
  411.2 21.8 %collective-permute-done.13 = bf16[256,2048]{1,0:T(8,128)(2,1)S(1)} collective-permute-done((bf16[256,2048]{1,0:T(8,128)(2,1)S(1)}, bf16[256,2048]{1,0:T(8,128)(2,1)S(1)}, u32[]{:S(2)}, u32[]{:S(2)}) %collective-permute-start.13) | collective-permute-done | bytes 1048608 | tf_op jit(solution)/shard_map/ppermute | solution.py:320
  443.1 13.1 %all_to_all.41 = bf16[4,320,256]{2,1,0:T(8,128)(2,1)S(1)} all-to-all(bf16[4,320,256]{2,1,0:T(8,128)(2,1)S(1)} %bitcast.191), channel_id=1, replica_groups=mesh['sh'=4,'sl'=2,'kh'=2,'kl'=2] {'kh','kl'}, dimensions={0} | all-to-all | bytes 1310720 | tf_op jit(solution)/shard_map/all_to_all | solution.py:451
  456.4 14.9 %attention_backward.1 = (bf16[320,1024]{1,0:T(8,128)(2,1)S(1)}, bf16[2,64,1024]{2,1,0:T(8,128)(2,1)S(1)}, bf16[2,64,1024]{2,1,0:T(8,128)(2,1)S(1)}, f32[64,1]{1,0:T(8,128)S(1)}, f32[64,1]{1,0:T(8,128)S(1)}) custom-call(s32[5]{0:T(128)S(1)} %and_select_fusion.group_ref, f32[576,1024]{1,0:T(8,128)S(1)} %fusion.68.qp_ref.kp_ref.vp_ref, ...), custom_call_target="tpu_custom_call" | custom-call | flops 1677721600 | bytes 10000000 | tf_op jit(solution)/shard_map/attention_backward/pallas_call | solution.py:244
  477.1 10.9 %convolution_convert_fusion.2 = bf16[2048,1408]{1,0:T(8,128)(2,1)} fusion(bf16[1024,1408]{1,0:T(8,128)(2,1)S(1)} %copy-done.49, bf16[256,2048]{1,0:T(8,128)(2,1)} %collective-permute-done.8, bf16[256,2048]{1,0:T(8,128)(2,1)} %collective-permute-done.7, bf16[256,2048]{1,0:T(8,128)(2,1)} %collective-permute-done.6, bf16[256,2048]{1,0:T(8,128)(2,1)} %multiply_convert_fusion.3), kind=kOutput, calls=%fused_computation.7 | convolution fusion | flops 5925240832 | bytes 12845056 | tf_op jit(solution)/shard_map/dot_general | solution.py:48
  510.3 30.5 %collective-permute-done.22 = bf16[8,40,2048]{2,1,0:T(8,128)(2,1)S(1)} collective-permute-done((bf16[8,40,2048]{2,1,0:T(8,128)(2,1)S(1)}, bf16[8,40,2048]{2,1,0:T(8,128)(2,1)S(1)}, u32[]{:S(2)}, u32[]{:S(2)}) %collective-permute-start.22) | collective-permute-done | bytes 1310752 | tf_op jit(solution)/shard_map/ppermute | solution.py:320
  542.6 11.0 %convolution_convert_fusion.1 = bf16[2048,1408]{1,0:T(8,128)(2,1)} fusion(bf16[1024,1408]{1,0:T(8,128)(2,1)} %copy-done.50, bf16[256,2048]{1,0:T(8,128)(2,1)} %collective-permute-done.8, bf16[256,2048]{1,0:T(8,128)(2,1)} %collective-permute-done.7, bf16[256,2048]{1,0:T(8,128)(2,1)} %collective-permute-done.6, bf16[256,2048]{1,0:T(8,128)(2,1)} %multiply_convert_fusion.3), kind=kOutput, calls=%fused_computation.6 | convolution fusion | flops 5925240832 | bytes 12845056 | tf_op jit(solution)/shard_map/dot_general | solution.py:48
  553.9 11.0 %convolution_convert_fusion = bf16[2048,1408]{1,0:T(8,128)(2,1)} fusion(bf16[1024,1408]{1,0:T(8,128)(2,1)} %get-tuple-element.43, bf16[256,2048]{1,0:T(8,128)(2,1)} %collective-permute-done.17, bf16[256,2048]{1,0:T(8,128)(2,1)} %collective-permute-done.16, bf16[256,2048]{1,0:T(8,128)(2,1)} %collective-permute-done.15, bf16[256,2048]{1,0:T(8,128)(2,1)} %fusion.24), kind=kOutput, calls=%fused_computation.5 | convolution fusion | flops 5925240832 | bytes 12845056 | tf_op jit(solution)/shard_map/dot_general | solution.py:48
  579.4 46.9 %all-to-all-done.4 = bf16[4,256,2048]{2,1,0:T(8,128)(2,1)} async-done(((bf16[4,256,2048]{2,1,0:T(8,128)(2,1)}), bf16[4,256,2048]{2,1,0:T(8,128)(2,1)}, u32[]{:S(2)}, u32[]{:S(2)}) %all-to-all-start.4) | async-done | bytes 4194336 | tf_op jit(solution)/shard_map/all_to_all | solution.py:481
  664.0 13.9 %reduce-scatter.8.cloned.1.call-done = bf16[40,2048]{1,0:T(8,128)(2,1)} async-done(((bf16[320,2048]{1,0:T(8,128)(2,1)}), bf16[40,2048]{1,0:T(8,128)(2,1)}) %reduce-scatter.8.cloned.1.call-update) | async-done | bytes 163856 | tf_op jit(solution)/shard_map/reduce_scatter | solution.py:501
  680.9 62.9 %reduce-scatter.12.cloned.1.call-done = bf16[256,1408]{1,0:T(8,128)(2,1)} async-done(((bf16[2048,1408]{1,0:T(8,128)(2,1)}), bf16[256,1408]{1,0:T(8,128)(2,1)}) %reduce-scatter.12.cloned.1.call-update) | async-done | bytes 720912 | tf_op jit(solution)/shard_map/reduce_scatter | solution.py:431
  750.7 58.5 %reduce-scatter.14.cloned.1.call-done = bf16[256,1408]{1,0:T(8,128)(2,1)} async-done(((bf16[2048,1408]{1,0:T(8,128)(2,1)}), bf16[256,1408]{1,0:T(8,128)(2,1)}) %reduce-scatter.14.cloned.1.call-update) | async-done | bytes 720912 | tf_op jit(solution)/shard_map/reduce_scatter | solution.py:431
  (272 shorter events, 258.9 us)
Async XLA Ops:
  7.2 108.8 %all-gather.8.cloned.1.call-start = ((), (), s32[]{:S(2)}) async-start(), calls=%async_computation.13 | async-start | bytes 1474560 | tf_op jit(solution)/shard_map/all_gather | solution.py:365
  9.0 170.0 %all-gather.6.cloned.1.call-start = ((), (), s32[]{:S(2)}) async-start(), calls=%async_computation.12 | async-start | bytes 2949120 | tf_op jit(solution)/shard_map/all_gather | solution.py:357
  21.5 200.5 %all-gather.14.cloned.1.call-start = ((), (), s32[]{:S(2)}) async-start(), calls=%async_computation.16 | async-start | bytes 6488064 | tf_op jit(solution)/shard_map/all_gather | solution.py:368
  23.4 243.5 %all-gather.12.cloned.1.call-start = ((), (), s32[]{:S(2)}) async-start(), calls=%async_computation.15 | async-start | bytes 6488064 | tf_op jit(solution)/shard_map/all_gather | solution.py:367
  26.7 80.9 %collective-permute-start = (bf16[256,2048]{1,0:T(8,128)(2,1)S(1)}, bf16[256,2048]{1,0:T(8,128)(2,1)}, u32[]{:S(2)}, u32[]{:S(2)}) collective-permute-start(bf16[256,2048]{1,0:T(8,128)(2,1)S(1)} %copy-done.15), channel_id=1, source_target_pairs={{0,1},{1,0},{2,3},{3,2},{4,5},{5,4},{6,7},{7,6},{8,9},{9,8},{10,11... | collective-permute-start | bytes 3145736 | tf_op jit(solution)/shard_map/ppermute | solution.py:320
  56.6 54.7 %collective-permute-start.1 = (bf16[256,2048]{1,0:T(8,128)(2,1)S(1)}, bf16[256,2048]{1,0:T(8,128)(2,1)}, u32[]{:S(2)}, u32[]{:S(2)}) collective-permute-start(bf16[256,2048]{1,0:T(8,128)(2,1)S(1)} %copy-done.15), channel_id=1, source_target_pairs={{0,2},{1,3},{2,0},{3,1},{4,6},{5,7},{6,4},{7,5},{8,10},{9,11},{10,... | collective-permute-start | bytes 3145736 | tf_op jit(solution)/shard_map/ppermute | solution.py:320
  58.1 55.6 %collective-permute-start.2 = (bf16[256,2048]{1,0:T(8,128)(2,1)S(1)}, bf16[256,2048]{1,0:T(8,128)(2,1)}, u32[]{:S(2)}, u32[]{:S(2)}) collective-permute-start(bf16[256,2048]{1,0:T(8,128)(2,1)S(1)} %copy-done.15), channel_id=1, source_target_pairs={{0,3},{1,2},{2,1},{3,0},{4,7},{5,6},{6,5},{7,4},{8,11},{9,10},{10,... | collective-permute-start | bytes 3145736 | tf_op jit(solution)/shard_map/ppermute | solution.py:320
  63.7 233.6 %all-gather.10.cloned.1.call-start = ((), (), s32[]{:S(2)}) async-start(), calls=%async_computation.14 | async-start | bytes 6488064 | tf_op jit(solution)/shard_map/all_gather | solution.py:366
  68.1 152.4 %collective-permute-start.17 = (bf16[256,2048]{1,0:T(8,128)(2,1)}, bf16[256,2048]{1,0:T(8,128)(2,1)}, u32[]{:S(2)}, u32[]{:S(2)}) collective-permute-start(bf16[256,2048]{1,0:T(8,128)(2,1)} %fusion.24), channel_id=1, source_target_pairs={{0,6},{1,7},{2,4},{3,5},{4,2},{5,3},{6,0},{7,1},{8,14},{9,15},{10,... | collective-permute-start | bytes 3145736 | tf_op jit(solution)/shard_map/ppermute | solution.py:320
  105.9 116.1 %collective-permute-start.16 = (bf16[256,2048]{1,0:T(8,128)(2,1)}, bf16[256,2048]{1,0:T(8,128)(2,1)}, u32[]{:S(2)}, u32[]{:S(2)}) collective-permute-start(bf16[256,2048]{1,0:T(8,128)(2,1)} %fusion.24), channel_id=1, source_target_pairs={{0,2},{1,3},{2,0},{3,1},{4,6},{5,7},{6,4},{7,5},{8,10},{9,11},{10,... | collective-permute-start | bytes 3145736 | tf_op jit(solution)/shard_map/ppermute | solution.py:320
  107.6 114.5 %collective-permute-start.15 = (bf16[256,2048]{1,0:T(8,128)(2,1)}, bf16[256,2048]{1,0:T(8,128)(2,1)}, u32[]{:S(2)}, u32[]{:S(2)}) collective-permute-start(bf16[256,2048]{1,0:T(8,128)(2,1)} %fusion.24), channel_id=1, source_target_pairs={{0,4},{1,5},{2,6},{3,7},{4,0},{5,1},{6,2},{7,3},{8,12},{9,13},{10,... | collective-permute-start | bytes 3145736 | tf_op jit(solution)/shard_map/ppermute | solution.py:320
  116.0 61.8 %collective-permute-start.3 = (bf16[8,1,40,2048]{3,2,1,0:T(8,128)(2,1)}, bf16[8,1,40,2048]{3,2,1,0:T(8,128)(2,1)S(1)}, u32[]{:S(2)}, u32[]{:S(2)}) collective-permute-start(bf16[8,1,40,2048]{3,2,1,0:T(8,128)(2,1)} %bitcast.188), channel_id=1, source_target_pairs={{0,1},{1,0},{2,3},{3,2},{4,5},{5,4},{6,7},{7,6},{8,9},{9,8},{10,11... | collective-permute-start | bytes 3932168 | tf_op jit(solution)/shard_map/ppermute | solution.py:320
  116.0 61.8 %collective-permute-start.4 = (bf16[8,1,40,2048]{3,2,1,0:T(8,128)(2,1)}, bf16[8,1,40,2048]{3,2,1,0:T(8,128)(2,1)}, u32[]{:S(2)}, u32[]{:S(2)}) collective-permute-start(bf16[8,1,40,2048]{3,2,1,0:T(8,128)(2,1)} %bitcast.189), channel_id=1, source_target_pairs={{0,2},{1,3},{2,0},{3,1},{4,6},{5,7},{6,4},{7,5},{8,10},{9,11},{10,... | collective-permute-start | bytes 3932168 | tf_op jit(solution)/shard_map/ppermute | solution.py:320
  201.0 441.4 %reduce-scatter.6.cloned.1.call-start = ((), (), s32[]{:S(2)}) async-start(), calls=%async_computation.17 | async-start | bytes 2654208 | tf_op jit(solution)/shard_map/reduce_scatter | solution.py:463
  353.3 57.8 %collective-permute-start.14 = (bf16[256,2048]{1,0:T(8,128)(2,1)S(1)}, bf16[256,2048]{1,0:T(8,128)(2,1)S(1)}, u32[]{:S(2)}, u32[]{:S(2)}) collective-permute-start(bf16[256,2048]{1,0:T(8,128)(2,1)S(1)} %get-tuple-element.48), channel_id=1, source_target_pairs={{0,6},{1,7},{2,4},{3,5},{4,2},{5,3},{6,0},{7,1},{8,14},{9,15},{10,... | collective-permute-start | bytes 3145736 | tf_op jit(solution)/shard_map/ppermute | solution.py:320
  355.8 77.2 %collective-permute-start.13 = (bf16[256,2048]{1,0:T(8,128)(2,1)S(1)}, bf16[256,2048]{1,0:T(8,128)(2,1)S(1)}, u32[]{:S(2)}, u32[]{:S(2)}) collective-permute-start(bf16[256,2048]{1,0:T(8,128)(2,1)S(1)} %get-tuple-element.49), channel_id=1, source_target_pairs={{0,2},{1,3},{2,0},{3,1},{4,6},{5,7},{6,4},{7,5},{8,10},{9,11},{10,... | collective-permute-start | bytes 3145736 | tf_op jit(solution)/shard_map/ppermute | solution.py:320
  366.2 66.8 %collective-permute-start.12 = (bf16[256,2048]{1,0:T(8,128)(2,1)S(1)}, bf16[256,2048]{1,0:T(8,128)(2,1)S(1)}, u32[]{:S(2)}, u32[]{:S(2)}) collective-permute-start(bf16[256,2048]{1,0:T(8,128)(2,1)S(1)} %get-tuple-element.47), channel_id=1, source_target_pairs={{0,4},{1,5},{2,6},{3,7},{4,0},{5,1},{6,2},{7,3},{8,12},{9,13},{10,... | collective-permute-start | bytes 3145736 | tf_op jit(solution)/shard_map/ppermute | solution.py:320
  477.0 180.1 %reduce-scatter.10.cloned.1.call-start = ((), (), s32[]{:S(2)}) async-start(), calls=%async_computation.19 | async-start | bytes 6488064 | tf_op jit(solution)/shard_map/reduce_scatter | solution.py:431
  488.0 190.0 %reduce-scatter.8.cloned.1.call-start = ((), (), s32[]{:S(2)}) async-start(), calls=%async_computation.18 | async-start | bytes 1474560 | tf_op jit(solution)/shard_map/reduce_scatter | solution.py:501
  542.5 201.3 %reduce-scatter.12.cloned.1.call-start = ((), (), s32[]{:S(2)}) async-start(), calls=%async_computation.20 | async-start | bytes 6488064 | tf_op jit(solution)/shard_map/reduce_scatter | solution.py:431
  553.6 255.6 %reduce-scatter.14.cloned.1.call-start = ((), (), s32[]{:S(2)}) async-start(), calls=%async_computation.21 | async-start | bytes 6488064 | tf_op jit(solution)/shard_map/reduce_scatter | solution.py:431
  573.1 53.2 %all-to-all-start.4 = ((bf16[4,256,2048]{2,1,0:T(8,128)(2,1)}), bf16[4,256,2048]{2,1,0:T(8,128)(2,1)}, u32[]{:S(2)}, u32[]{:S(2)}) async-start(bf16[4,256,2048]{2,1,0:T(8,128)(2,1)} %bitcast.186), calls=%async_computation.4 | async-start | bytes 8388608 | tf_op jit(solution)/shard_map/all_to_all | solution.py:481
  657.2 154.3 %collective-permute-start.23 = (bf16[256,1408]{1,0:T(8,128)(2,1)}, bf16[256,1408]{1,0:T(8,128)(2,1)}, u32[]{:S(2)}, u32[]{:S(2)}) collective-permute-start(bf16[256,1408]{1,0:T(8,128)(2,1)} %reduce-scatter.10.cloned.1.call-done), channel_id=1, source_target_pairs={{0,0},{1,4},{2,2},{3,6},{4,1},{5,5},{6,3},{7,7},{8,8},{9,12},{10,1... | collective-permute-start | bytes 2162696 | tf_op jit(solution)/shard_map/ppermute | solution.py:320
  743.8 72.2 %collective-permute-start.24 = (bf16[256,1408]{1,0:T(8,128)(2,1)}, bf16[256,1408]{1,0:T(8,128)(2,1)}, u32[]{:S(2)}, u32[]{:S(2)}) collective-permute-start(bf16[256,1408]{1,0:T(8,128)(2,1)} %reduce-scatter.12.cloned.1.call-done), channel_id=1, source_target_pairs={{0,0},{1,4},{2,2},{3,6},{4,1},{5,5},{6,3},{7,7},{8,8},{9,12},{10,1... | collective-permute-start | bytes 2162696 | tf_op jit(solution)/shard_map/ppermute | solution.py:320
  (70 other events, 1352.8 us)
Sparse Core Ops, SparseCore 0:
  10.8 46.6 all-gather.7
  59.6 53.9 all-gather.5
  115.8 58.9 all-gather.13
  176.9 59.0 all-gather.11
  238.1 59.0 all-gather.9
  477.1 67.2 reduce-scatter.5
  546.7 63.9 reduce-scatter.9
  614.7 63.2 reduce-scatter.7
  680.3 63.4 reduce-scatter.11
  746.0 63.1 reduce-scatter.13

commit v2 on v1

--- a/solution.py
+++ b/solution.py
@@ -269,6 +269,56 @@
     )(groups, mixed, mixed, query_rows, key_rows, value_rows, grads, lse, cosine, sine, gain_q, gain_k)
 
 
+def block_order_kernel(mine_ref, in_ref, out_ref, *, offsets, back, columns):
+    mine = mine_ref[0]
+    for index, offset in enumerate(offsets):
+        held = mine ^ offset
+        if columns:
+            width = in_ref.shape[1] // len(offsets)
+            held = pl.ds(pl.multiple_of(held * width, width), width)
+            here = slice(index * width, (index + 1) * width)
+            if back:
+                out_ref[:, held] = in_ref[:, here]
+            else:
+                out_ref[:, here] = in_ref[:, held]
+        elif back:
+            out_ref[held] = in_ref[index]
+        else:
+            out_ref[index] = in_ref[held]
+
+
+def block_order(array, mine, offsets, back=False, columns=False):
+    if columns and array.shape[1] // len(offsets) % 128:
+        width = array.shape[1] // len(offsets)
+        sources = [mine ^ offset for offset in offsets]
+        if back:
+            place = {offset: index for index, offset in enumerate(offsets)}
+            table = jnp.array([place[v] for v in range(len(offsets))], jnp.int32)
+            sources = [
+                jnp.sum(jnp.where(jnp.arange(len(offsets)) == (mine ^ j), table, 0))
+                for j in range(len(offsets))
+            ]
+        return jnp.concatenate(
+            [lax.dynamic_slice_in_dim(array, at * width, width, 1) for at in sources], axis=1
+        )
+    return pl.pallas_call(
+        functools.partial(
+            block_order_kernel, offsets=tuple(offsets), back=back, columns=columns
+        ),
+        name="block_order",
+        out_shape=jax.ShapeDtypeStruct(array.shape, array.dtype),
+        in_specs=[
+            pl.BlockSpec(memory_space=pltpu.SMEM),
+            pl.BlockSpec(memory_space=pltpu.VMEM),
+        ],
+        out_specs=pl.BlockSpec(memory_space=pltpu.VMEM),
+        compiler_params=pltpu.CompilerParams(vmem_limit_bytes=VMEM_LIMIT),
+        cost_estimate=pl.CostEstimate(
+            flops=0, transcendentals=0, bytes_accessed=4 * array.size
+        ),
+    )(mine.reshape(1).astype(jnp.int32), array)
+
+
 def adamw(weight, grad, first, second, rate, shrink, item_count):
     first_new = beta_first * first + (1.0 - beta_first) * grad
     second_new = beta_second * second + (1.0 - beta_second) * grad * grad
@@ -328,6 +378,28 @@
     def in_sequence(array, r):
         return permute(array, lambda sh, sl, kh, kl: (sh, sl, kh ^ (r >> 1), kl ^ (r & 1)))
 
+    def along_z(array, r):
+        return permute(array, lambda sh, sl, kh, kl: (sh ^ r, sl, kh, kl))
+
+    def along_y(array):
+        return permute(array, lambda sh, sl, kh, kl: (sh, sl ^ 1, kh, kl))
+
+    z_size = sizes[0]
+
+    def gather_line(piece):
+        return jnp.stack([piece] + [along_z(piece, r) for r in range(1, z_size)])
+
+    def halve(blocks, index, axis, move):
+        kept = lax.dynamic_index_in_dim(blocks, index, axis, keepdims=False)
+        sent = lax.dynamic_index_in_dim(blocks, index ^ 1, axis, keepdims=False)
+        return kept.astype(high) + move(sent.astype(low)).astype(high)
+
+    def scatter_line(line):
+        total = line[0]
+        for r in range(1, z_size):
+            total = total + along_z(line[r].astype(low), r).astype(high)
+        return total
+
     item_count, model = tokens.shape
     heads = QUERY_HEADS // parts
     width = heads * HEAD_SIZE
@@ -339,7 +411,24 @@
     cosine, sine = angle_tables(length)
     groups = ((jnp.arange(heads, dtype=jnp.int32) + kv) // 4).astype(jnp.int32)
 
+    def stage(ready, waiting):
+        return lax.optimization_barrier((ready, waiting))
+
+    column_offsets = [rz * 2 + rs for rs in range(2) for rz in range(z_size)]
+    row_offsets = [
+        (rz * 2 + rs) * parts + r for r in range(parts) for rs in range(2) for rz in range(z_size)
+    ]
+
+    def columns_moved(array, back=False):
+        return block_order(array, lax.axis_index(SEQ), column_offsets, back=back, columns=True)
+
+    def rows_moved(array, back=False):
+        blocks = array.reshape(devices, -1, item_count)
+        return block_order(blocks, lax.axis_index(ALL), row_offsets, back=back).reshape(-1, item_count)
+
+    gate_block = swap(gate_weight.astype(low))
     qkv_low = qkv_weight.astype(low)
+    span = width + 2 * pair
     qkv_parts = jnp.stack(
         [
             jnp.concatenate(
@@ -354,39 +443,55 @@
         ]
     )
     qkv_rows = lax.all_to_all(qkv_parts, KV, split_axis=0, concat_axis=0, tiled=True)
-    qkv_full = lax.all_gather(
-        qkv_rows.reshape(-1, width + 2 * pair), SEQ, axis=0, tiled=True
-    )
-    gains_low = lax.all_to_all(
-        jnp.broadcast_to(gains.astype(low)[None], (devices, gains.shape[0])),
-        ALL, split_axis=0, concat_axis=0, tiled=True,
-    ).reshape(-1)
-    gain_values = gains_low.astype(high)
-    out_rows = lax.all_gather(out_weight.astype(low), SEQ, axis=0, tiled=True)
-    gate_full = lax.all_gather(swap(gate_weight.astype(low)), OWNERS, axis=0, tiled=True)
-    up_full = lax.all_gather(swap(up_weight.astype(low)), OWNERS, axis=0, tiled=True)
-    down_full = lax.all_gather(swap(down_weight.astype(low)), OWNERS, axis=0, tiled=True)
-
-    all_rows = jnp.zeros((parts, item_count, model), low)
-    all_rows = lax.dynamic_update_slice_in_dim(all_rows, tokens[None], kv, 0)
-    for r in range(1, parts):
-        all_rows = lax.dynamic_update_slice_in_dim(
-            all_rows, in_sequence(tokens, r)[None], kv ^ r, 0
-        )
-    all_rows = all_rows.reshape(length, model).astype(high)
-    normed = (all_rows * rms_scale(all_rows) * gain_values[:model]).astype(low)
-
+    moved_tokens = columns_moved(tokens)
+    tokens_far = in_sequence(moved_tokens, 2)
     factor = jnp.sum(
         jnp.where(jnp.arange(corpus_weight.shape[0]) == corpus_id[0], corpus_weight, 0.0)
     )
     weighted = cotangent.astype(high) * factor
-    weighted_low = weighted.astype(low)
-    weighted_rows = jnp.concatenate(
-        [weighted_low] + [in_ffn_group(weighted_low, r) for r in range(1, 4)], axis=0
-    )
-
+    (gate_block, qkv_rows, tokens_far), (up_low, down_low, out_low, tokens_near, weighted_low, gains_own) = stage(
+        (gate_block, qkv_rows, tokens_far),
+        (
+            up_weight.astype(low), down_weight.astype(low), out_weight.astype(low), moved_tokens,
+            weighted.astype(low), gains,
+        ),
+    )
+
+    qkv_line = gather_line(qkv_rows.reshape(-1, span))
+    out_line = gather_line(out_low)
+    up_block = swap(up_low)
+    down_block = swap(down_low)
+    tokens_pair = (in_sequence(tokens_near, 1), in_sequence(tokens_far, 1))
+    gains_low = lax.all_to_all(
+        jnp.broadcast_to(gains_own.astype(low)[None], (devices, gains.shape[0])),
+        ALL, split_axis=0, concat_axis=0, tiled=True,
+    )
+    weighted_far = in_ffn_group(weighted_low, 2)
+    (qkv_line, out_line, tokens_pair, gains_low), (gate_block,) = stage(
+        (qkv_line, out_line, tokens_pair, gains_low), (gate_block,)
+    )
+    gate_full = lax.all_gather(gate_block, OWNERS, axis=0, tiled=True)
+    gain_values = gains_low.reshape(-1).astype(high)
+    gain_one = gain_values[:model]
+    gain_two = gain_values[model : 2 * model]
     gain_q = gain_values[2 * model : 2 * model + HEAD_SIZE].reshape(HEAD_SIZE, 1)
     gain_k = gain_values[2 * model + HEAD_SIZE :].reshape(HEAD_SIZE, 1)
+    gain_moved = columns_moved(jnp.broadcast_to(gain_one[None], (8, model)))[:1]
+    all_rows = jnp.zeros((parts, item_count, model), low)
+    for r, piece in enumerate((tokens_near, tokens_pair[0], tokens_far, tokens_pair[1])):
+        all_rows = lax.dynamic_update_slice_in_dim(all_rows, piece[None], kv ^ r, 0)
+    all_rows = all_rows.reshape(length, model).astype(high)
+    normed = (all_rows * rms_scale(all_rows) * gain_moved).astype(low)
+
+    qkv_far = along_y(qkv_line)
+    (qkv_far, weighted_far, normed), (out_line, up_block, weighted_low) = stage(
+        (qkv_far, weighted_far, normed), (out_line, up_block, weighted_low)
+    )
+    up_full = lax.all_gather(up_block, OWNERS, axis=0, tiled=True)
+    qkv_full = jnp.concatenate([qkv_line, qkv_far]).reshape(model, span)
+
+    out_near = jnp.stack([out_line, along_y(out_line)])
+    out_far = in_sequence(out_near, 2)
     mixed = contract(qkv_full, normed, 0, 1)
     query_rows, key_rows, value_rows, result, lse = attend(
         groups, mixed, cosine, sine, gain_q, gain_k, heads
@@ -394,24 +499,30 @@
     outgoing = jnp.stack(
         [result.reshape(width, length)[:, d * item_count : (d + 1) * item_count] for d in range(parts)]
     )
-    attended = lax.all_to_all(outgoing, KV, split_axis=0, concat_axis=0, tiled=True).reshape(
-        parts * width, item_count
-    )
-
-    out_near = out_rows.reshape(seqs, 1, -1, model)
-    out_far = in_sequence(out_near, 2)
-    out_full = jnp.zeros((seqs, parts) + out_near.shape[2:], low)
-    for r, piece in enumerate((out_near, in_sequence(out_near, 1), out_far, in_sequence(out_far, 1))):
-        out_full = lax.dynamic_update_slice_in_dim(out_full, piece, kv ^ r, 1)
-    out_full = out_full.reshape(-1, model)
+    out_far, (outgoing, out_near, weighted_low, weighted_far, down_block) = stage(
+        out_far, (outgoing, out_near, weighted_low, weighted_far, down_block)
+    )
+    down_full = lax.all_gather(down_block, OWNERS, axis=0, tiled=True)
+
+    attended = rows_moved(
+        lax.all_to_all(outgoing, KV, split_axis=0, concat_axis=0, tiled=True)
+    )
+    out_pair = (in_sequence(out_near, 1), in_sequence(out_far, 1))
+    out_full = jnp.stack([out_near, out_pair[0], out_far, out_pair[1]]).reshape(-1, model)
+    attended, weighted_low, weighted_far = lax.optimization_barrier(
+        (attended, weighted_low, weighted_far)
+    )
+    weighted_rows = jnp.concatenate(
+        [weighted_low, in_ffn_group(weighted_low, 1), weighted_far, in_ffn_group(weighted_far, 1)],
+        axis=0,
+    )
     inputs = tokens.astype(high)
     hidden = inputs + contract(attended, out_full, 0, 0)
 
     scale_two = rms_scale(hidden)
-    gain_two = gain_values[model : 2 * model]
     normed_two = (hidden * scale_two * gain_two).astype(low)
     ffn_rows = jnp.concatenate(
-        [normed_two] + [in_ffn_group(normed_two, r) for r in range(1, 4)], axis=0
+        [normed_two] + [in_ffn_group(normed_two, r) for r in (1, 2, 3)], axis=0
     )
     gate = contract(ffn_rows, gate_full, 1, 0)
     up_part = contract(ffn_rows, up_full, 1, 0)
@@ -419,39 +530,56 @@
     swish = gate * sigma
     acted = (swish * up_part).astype(low)
 
-    def to_owners(partial):
-        blocks = partial.reshape(4, item_count, model)
-        total = blocks[0]
-        for r in range(1, 4):
-            total = total + in_ffn_group(blocks[r].astype(low), r).astype(high)
-        return total
+    def from_group(sent):
+        return [
+            in_ffn_group(sent[(r - 1) * item_count : r * item_count], r) for r in (1, 2, 3)
+        ]
 
     def share(grad):
-        return swap(
-            lax.psum_scatter(grad.astype(low), OWNERS, scatter_dimension=0, tiled=True)
-        ).astype(high)
-
-    grad_down = share(contract(weighted_rows, acted, 0, 0))
+        return lax.psum_scatter(grad, OWNERS, scatter_dimension=0, tiled=True)
+
+    grad_down_low = contract(weighted_rows, acted, 0, 0).astype(low)
+    down_full, grad_down_low = stage(down_full, grad_down_low)
+    grad_down_share = share(grad_down_low)
     grad_acted = contract(weighted_rows, down_full, 1, 0)
     grad_gate = (grad_acted * up_part * sigma * (1.0 + gate * (1.0 - sigma))).astype(low)
     grad_up = (grad_acted * swish).astype(low)
-    grad_normed_two = to_owners(
-        contract(grad_gate, gate_full, 1, 1) + contract(grad_up, up_full, 1, 1)
-    )
-    grad_gate_w = share(contract(ffn_rows, grad_gate, 0, 0))
-    grad_up_w = share(contract(ffn_rows, grad_up, 0, 0))
-    ffn = to_owners(contract(acted, down_full, 1, 1))
-    block_out = (hidden + ffn).astype(low)
+    rows_partial = contract(grad_gate, gate_full, 1, 1) + contract(grad_up, up_full, 1, 1)
+    own_rows = rows_partial[:item_count]
+    (sent_rows, own_rows), (grad_gate, grad_up) = stage(
+        (rows_partial[item_count:].astype(low), own_rows), (grad_gate, grad_up)
+    )
+    received = from_group(sent_rows)
+    grad_gate_low = contract(ffn_rows, grad_gate, 0, 0).astype(low)
+    grad_up_low = contract(ffn_rows, grad_up, 0, 0).astype(low)
+    ffn_partial = contract(acted, down_full, 1, 1).astype(low)
+    received, (grad_gate_low, grad_up_low, ffn_partial) = stage(
+        received, (grad_gate_low, grad_up_low, ffn_partial)
+    )
+    grad_gate_share = share(grad_gate_low)
+    grad_up_share = share(grad_up_low)
+    grad_normed_two = own_rows + sum(piece.astype(high) for piece in received)
 
     pushed_two, gain_two_terms = norm_back(grad_normed_two, hidden, scale_two, gain_two)
     grad_hidden = weighted + pushed_two
     hidden_low = grad_hidden.astype(low)
 
-    attended_gradient = contract(out_full, hidden_low, 1, 1).astype(low)
+    attended_gradient = rows_moved(contract(out_full, hidden_low, 1, 1).astype(low), back=True)
     incoming = lax.all_to_all(
         attended_gradient.reshape(parts, width, item_count), KV, split_axis=0, concat_axis=0, tiled=True
     )
+    ffn_blocks = ffn_partial.reshape(2, 2, item_count, model)
+    ffn_line = [
+        ffn_blocks[r, 0].astype(high) + in_ffn_group(ffn_blocks[r, 1], 1).astype(high) for r in range(2)
+    ]
+    attended = attended.reshape(2, 2, -1, item_count)
+    sent_out = [contract(attended[r, 1], hidden_low, 1, 0).astype(low) for r in range(2)]
+    kept_out = [contract(attended[r, 0], hidden_low, 1, 0) for r in range(2)]
+    (incoming, kept_out), (sent_out,) = stage((incoming, kept_out), (sent_out,))
     grads = jnp.concatenate([incoming[d] for d in range(parts)], axis=1)
+
+    out_line = [kept_out[r] + in_sequence(sent_out[r], 1).astype(high) for r in range(2)]
+    out_line = out_line[0] + in_sequence(out_line[1].astype(low), 2).astype(high)
     grad_queries, grad_keys, grad_values, gain_q_sum, gain_k_sum = attend_back(
         groups, mixed, query_rows, key_rows, value_rows, grads, lse,
         cosine, sine, gain_q, gain_k, heads,
@@ -459,10 +587,37 @@
     grad_mixed = jnp.concatenate(
         [grad_queries, grad_keys.reshape(pair, length), grad_values.reshape(pair, length)], axis=0
     )
-    grad_mixer = contract(normed, grad_mixed, 0, 1).astype(low)
-    mixer_share = lax.psum_scatter(grad_mixer, SEQ, scatter_dimension=0, tiled=True)
+
+    half_model = model // 2
+    mixer_sent = contract(normed[:, half_model:], grad_mixed, 0, 1).astype(low)
+    mixer_line = contract(normed[:, :half_model], grad_mixed, 0, 1)
+    (mixer_sent, mixer_line), (grad_mixed, out_line, ffn_line) = stage(
+        (mixer_sent, mixer_line), (grad_mixed, out_line, ffn_line)
+    )
+    mixer_line = mixer_line + along_y(mixer_sent).astype(high)
+    out_line = out_line.reshape(2, z_size, -1, model)
+    out_line = out_line[0] + along_y(out_line[1].astype(low)).astype(high)
+    grad_normed = contract(grad_mixed, qkv_full, 0, 1).astype(low)
+    grad_normed = halve(
+        grad_normed.reshape(2, 2, item_count, model), lax.axis_index("kl"), 1, lambda v: in_sequence(v, 1)
+    )
+    (mixer_line, grad_normed), (ffn_line, grad_down_share, grad_gate_share) = stage(
+        (mixer_line, grad_normed), (ffn_line, grad_down_share, grad_gate_share)
+    )
+
+    mixer_share = scatter_line(mixer_line.reshape(z_size, -1, span)).astype(low)
+    out_grad = scatter_line(out_line)
+    grad_normed = halve(grad_normed, lax.axis_index("kh"), 0, lambda v: in_sequence(v, 2))
+    ffn = ffn_line[0] + in_ffn_group(ffn_line[1].astype(low), 2).astype(high)
+    block_out = (hidden + ffn).astype(low)
+    grad_down = swap(grad_down_share).astype(high)
+    grad_gate_w = swap(grad_gate_share).astype(high)
+    (mixer_share, grad_normed), (grad_up_share,) = stage(
+        (mixer_share, grad_normed), (grad_up_share,)
+    )
+
     mixer_parts = lax.all_to_all(
-        mixer_share.reshape(parts, -1, width + 2 * pair), KV, split_axis=0, concat_axis=0, tiled=True
+        mixer_share.reshape(parts, -1, span), KV, split_axis=0, concat_axis=0, tiled=True
     ).astype(high)
     slots = [[None] * VALUE_GROUPS, [None] * VALUE_GROUPS]
     for d in range(parts):
@@ -475,36 +630,17 @@
     qkv_grad = jnp.concatenate(
         [mixer_parts[d, :, :width] for d in range(parts)] + slots[0] + slots[1], axis=1
     )
-
-    grad_normed = contract(grad_mixed, qkv_full, 0, 1).astype(low)
-    grad_normed = jnp.sum(
-        lax.all_to_all(
-            grad_normed.reshape(parts, item_count, model), KV, split_axis=0, concat_axis=0, tiled=True
-        ).astype(high),
-        axis=0,
-    )
+    moved_inputs = tokens_near.astype(high)
     pushed_one, gain_one_terms = norm_back(
-        grad_normed, inputs, rms_scale(inputs), gain_values[:model]
-    )
-    grad_input = grad_hidden + pushed_one
-
-    grad_output = contract(attended, hidden_low, 1, 0)
-    blocks = grad_output.reshape(seqs, 2, 2, -1, model)
-    is_low = lax.axis_index("kl") == 0
-    kept = jnp.where(is_low, blocks[:, :, 0], blocks[:, :, 1])
-    sent = jnp.where(is_low, blocks[:, :, 1], blocks[:, :, 0]).astype(low)
-    blocks = kept + in_sequence(sent, 1).astype(high)
-    is_first = lax.axis_index("kh") == 0
-    kept = jnp.where(is_first, blocks[:, 0], blocks[:, 1])
-    sent = jnp.where(is_first, blocks[:, 1], blocks[:, 0]).astype(low)
-    blocks = kept + in_sequence(sent, 2).astype(high)
-    out_grad = lax.psum_scatter(
-        blocks.astype(low).reshape(-1, model), SEQ, scatter_dimension=0, tiled=True
-    ).astype(high)
-
+        grad_normed, moved_inputs, rms_scale(moved_inputs), gain_moved
+    )
+    grad_input = grad_hidden + columns_moved(pushed_one, back=True)
+    gain_one_sum = columns_moved(
+        jnp.broadcast_to(jnp.sum(gain_one_terms, 0)[None], (8, model)), back=True
+    )[0]
     grad_gains = jnp.concatenate(
         [
-            jnp.sum(gain_one_terms, 0),
+            gain_one_sum,
             jnp.sum(gain_two_terms, 0),
             gain_q_sum.reshape(-1),
             gain_k_sum.reshape(-1),
@@ -516,6 +652,7 @@
         ),
         axis=0,
     )
+    grad_up_w = swap(grad_up_share).astype(high)
 
     steps_done = step_count[0].astype(high)
     new_qkv, moments_qkv = adamw(qkv_weight, qkv_grad, first_qkv, second_qkv, 0.02, 0.1, steps_done)

time: 848 us -> 667 us (0.79)
  waiting for transfers between devices: 433 us -> 251 us
  matrix products: 139 us -> 125 us
  starting transfers between devices: 89 us -> 100 us
  other arithmetic: 68 us -> 76.5 us
    reduce_scatter x5 -> x3, waiting for transfers between devices: 135 us -> 0.02 us  [share(): return lax.psum_scatter(grad, OWNERS, scatter_dimension=0, tiled=True)]
    all_to_all x3, waiting for transfers between devices: 82.8 us -> 22.5 us  [the longest x1 14 us: local(): lax.all_to_all(qkv_parts, KV, split_axis=0, concat_axis=0, tiled=True)]
    ppermute x26 -> x45, waiting for transfers between devices: 188 us -> 219 us  [permute(): return lax.ppermute(array, ALL, pairs)]
    all_gather x5 -> x3, waiting for transfers between devices: 17.7 us -> 0.01 us  [the longest x1 0.01 us: local(): gate_full = lax.all_gather(gate_block, OWNERS, axis=0, tiled=True)]
    dot_general x15 -> x19, matrix products: 139 us -> 125 us  [contract(): lax.dot_general(left, right, (((left_dim,), (right_dim,)), ((), ())), pre...]
    dynamic_update_slice x8 -> x4, local copies, waits for them, and re-layouts: 15.6 us -> 6.78 us  [local(): all_rows = lax.dynamic_update_slice_in_dim(all_rows, piece[None], kv ^ r, 0)]
    ppermute x26 -> x45, starting transfers between devices: 68.1 us -> 74.9 us  [permute(): return lax.ppermute(array, ALL, pairs)]
    all_to_all x2 -> x1, blocking collectives: 23.9 us -> 18.8 us  [local(): lax.all_to_all(jnp.broadcast_to(gains_own.astype(low)[None], (devices, ga...]
  transfers between devices with their start and end apart: 41 -> 56, of which waited for: 19 -> 20; matrix products, arithmetic and copies ran while one was open for 20% -> 34% of each run, Pallas kernels for 1% -> 4%
where the time goes in v2:
time: 667 us; the launch traced here: 659 us
  waiting for transfers between devices  251 us (38%)
  matrix products  125 us (19%)
  starting transfers between devices  100 us (15%)
  other arithmetic  76.5 us (11%)
  local copies, waits for them, and re-layouts  43.3 us (6%)
  Pallas kernels  27 us (4%)
  blocking collectives  18.8 us (3%)
  between operations  17 us (3%)
    ppermute x45, waiting for transfers between devices, permute(): return lax.ppermute(array, ALL, pairs)  219 us
    dot_general x19, matrix products, contract(): lax.dot_general(left, right, (((left_dim,), (right_dim,)), ((), ())), pre...  125 us
    ppermute x45, starting transfers between devices, permute(): return lax.ppermute(array, ALL, pairs)  74.9 us
    another operation x12, other arithmetic, adamw(): jnp.stack([first_new, jnp.sqrt(second_new)])  21.8 us
    all_to_all x1, blocking collectives, local(): lax.all_to_all(jnp.broadcast_to(gains_own.astype(low)[None], (devices, ga...  18.8 us
    unnamed x171, local copies, waits for them, and re-layouts  16.7 us
    pallas_call x1, Pallas kernels, attend_back(): pl.pallas_call(functools.partial(backward_kernel, block=min(256, length))...  15.3 us
    all_to_all x1, waiting for transfers between devices, local(): lax.all_to_all(qkv_parts, KV, split_axis=0, concat_axis=0, tiled=True)  14 us
  transfers between devices with their start and end apart: 56, of which 20 were waited for; matrix products, arithmetic and copies ran while one was open for 34% of the time, Pallas kernels for 4%

profile of v2, /device:TPU:0, one launch (start us, length us, event | category | flops | bytes accessed | tf_op | source)
XLA Modules:
  0.0 659.3 jit_solution(13611098805372288025)
XLA Ops:
  29.5 14.0 %all-to-all-done = bf16[4,64,576]{2,1,0:T(8,128)(2,1)S(1)} async-done(((bf16[4,64,576]{2,1,0:T(8,128)(2,1)}), bf16[4,64,576]{2,1,0:T(8,128)(2,1)S(1)}, u32[]{:S(2)}, u32[]{:S(2)}) %all-to-all-start) | async-done | bytes 294944 | tf_op jit(solution)/shard_map/all_to_all | solution.py:445
  56.6 13.0 %collective-permute-done.6 = bf16[40,2048]{1,0:T(8,128)(2,1)S(1)} collective-permute-done((bf16[40,2048]{1,0:T(8,128)(2,1)S(1)}, bf16[40,2048]{1,0:T(8,128)(2,1)S(1)}, u32[]{:S(2)}, u32[]{:S(2)}) %collective-permute-start.6) | collective-permute-done | bytes 163872 | tf_op jit(solution)/shard_map/ppermute | solution.py:370
  72.7 18.8 %all_to_all.38 = bf16[32,1,132]{2,1,0:T(2,128)(2,1)S(1)} all-to-all(bf16[32,1,132]{2,1,0:T(2,128)(2,1)S(1)} %broadcast_in_dim.21), channel_id=1, replica_groups=mesh['sh'=4,'sl'=2,'kh'=2,'kl'=2] {'sh','sl','kh','kl'}, dimensions={0} | all-to-all | bytes 16896 | tf_op jit(solution)/shard_map/all_to_all | solution.py:465
  121.6 13.4 %collective-permute-done.10 = bf16[4,256,576]{1,2,0:T(8,128)(2,1)} collective-permute-done((bf16[4,256,576]{1,2,0:T(8,128)(2,1)}, bf16[4,256,576]{1,2,0:T(8,128)(2,1)}, u32[]{:S(2)}, u32[]{:S(2)}) %collective-permute-start.10) | collective-permute-done | bytes 1179680 | tf_op jit(solution)/shard_map/ppermute | solution.py:370
  160.3 10.4 %attention_forward.1 = (bf16[5,64,1024]{2,1,0:T(8,128)(2,1)S(1)}, bf16[2,64,1024]{2,1,0:T(8,128)(2,1)S(1)}, bf16[2,64,1024]{2,1,0:T(8,128)(2,1)S(1)}, bf16[5,64,1024]{2,1,0:T(8,128)(2,1)S(1)}, f32[5,1,1024]{2,1,0:T(1,128)S(1)}) custom-call(s32[5]{0:T(128)S(1)} %and_select_fusion.group_ref, f32[576,1024]{1,0:T(8,128)S(1)} %fusion.58.qp_ref.kp_ref.vp_ref, ...), custom_call_target="tpu_custom_call" | custom-call | flops 671088640 | bytes 8000000 | tf_op jit(solution)/shard_map/attention_forward/pallas_call | solution.py:217
  172.4 11.5 %collective-permute-done.14 = bf16[2,4,40,2048]{3,2,1,0:T(8,128)(2,1)} collective-permute-done((bf16[2,4,40,2048]{3,2,1,0:T(8,128)(2,1)}, bf16[2,4,40,2048]{3,2,1,0:T(8,128)(2,1)}, u32[]{:S(2)}, u32[]{:S(2)}) %collective-permute-start.14) | collective-permute-done | bytes 1310752 | tf_op jit(solution)/shard_map/ppermute | solution.py:370
  189.2 8.9 %all-to-all-done.2 = bf16[4,320,256]{2,1,0:T(8,128)(2,1)S(1)} async-done(((bf16[4,320,256]{2,1,0:T(8,128)(2,1)}), bf16[4,320,256]{2,1,0:T(8,128)(2,1)S(1)}, u32[]{:S(2)}, u32[]{:S(2)}) %all-to-all-start.2) | async-done | bytes 655392 | tf_op jit(solution)/shard_map/all_to_all | solution.py:508
  209.7 37.6 %collective-permute-done.18 = bf16[256,2048]{1,0:T(8,128)(2,1)S(1)} collective-permute-done((bf16[256,2048]{1,0:T(8,128)(2,1)}, bf16[256,2048]{1,0:T(8,128)(2,1)S(1)}, u32[]{:S(2)}, u32[]{:S(2)}) %collective-permute-start.18) | collective-permute-done | bytes 1048608 | tf_op jit(solution)/shard_map/ppermute | solution.py:370
  248.6 21.1 %collective-permute-done.19 = bf16[256,2048]{1,0:T(8,128)(2,1)S(1)} collective-permute-done((bf16[256,2048]{1,0:T(8,128)(2,1)}, bf16[256,2048]{1,0:T(8,128)(2,1)S(1)}, u32[]{:S(2)}, u32[]{:S(2)}) %collective-permute-start.19) | collective-permute-done | bytes 1048608 | tf_op jit(solution)/shard_map/ppermute | solution.py:370
  272.7 18.6 %collective-permute-done.20 = bf16[256,2048]{1,0:T(8,128)(2,1)} collective-permute-done((bf16[256,2048]{1,0:T(8,128)(2,1)S(1)}, bf16[256,2048]{1,0:T(8,128)(2,1)}, u32[]{:S(2)}, u32[]{:S(2)}) %collective-permute-start.20) | collective-permute-done | bytes 1048608 | tf_op jit(solution)/shard_map/ppermute | solution.py:370
  291.4 12.9 %fusion.50 = f32[1024,1408]{1,0:T(8,128)} fusion(bf16[2048,1408]{1,0:T(8,128)(2,1)} %all-gather.6.cloned.1.call-done, bf16[256,2048]{1,0:T(8,128)(2,1)S(1)} %collective-permute-done.22, bf16[256,2048]{1,0:T(8,128)(2,1)} %copy-done.75, bf16[256,2048]{1,0:T(8,128)(2,1)} %collective-permute-done.20, bf16[256,2048]{1,0:T(8,128)(2,1)S(1)} %multiply_convert_fusion.3), kind=kOutput, calls=%fused_computation.185 | convolution fusion | flops 5922357248 | bytes 15728640 | tf_op jit(solution)/shard_map/dot_general | solution.py:48
  304.3 14.1 %multiply_convert_fusion.2 = (bf16[1024,1408]{1,0:T(8,128)(2,1)S(1)}, f32[1024,1408]{1,0:T(8,128)}) fusion(f32[1024,1408]{1,0:T(8,128)} %fusion.50, bf16[2048,1408]{1,0:T(8,128)(2,1)} %all-gather.8.cloned.1.call-done, bf16[256,2048]{1,0:T(8,128)(2,1)S(1)} %collective-permute-done.22, bf16[256,2048]{1,0:T(8,128)(2,1)} %copy-done.75, ...), kind=kOutput, calls=%fused_computation.10 | convolution fusion | flops 5931008000 | bytes 24379392 | tf_op jit(solution)/shard_map/dot_general | solution.py:48
  328.6 14.5 %multiply_convert_fusion.1 = (bf16[1024,1408]{1,0:T(8,128)(2,1)S(1)}, bf16[1024,1408]{1,0:T(8,128)(2,1)S(1)}) fusion(f32[1024,1408]{1,0:T(8,128)} %fusion.50, f32[1024,1408]{1,0:T(8,128)} %get-tuple-element.240, bf16[1024,2048]{1,0:T(8,128)(2,1)} %copy-done.63, bf16[2048,1408]{1,0:T(8,128)(2,1)} %all-gather.4.cloned.1.call-done), kind=kOutput, calls=%fused_computation.9 | convolution fusion | flops 5924323328 | bytes 27262976 | tf_op jit(solution)/shard_map/dot_general | solution.py:48
  343.1 9.8 %fusion.59 = f32[1024,2048]{1,0:T(8,128)S(1)} fusion(bf16[1024,1408]{1,0:T(8,128)(2,1)S(1)} %get-tuple-element.124, bf16[2048,1408]{1,0:T(8,128)(2,1)} %all-gather.8.cloned.1.call-done), kind=kOutput, calls=%fused_computation.193 | convolution fusion | flops 5905580032 | bytes 17039360 | tf_op jit(solution)/shard_map/dot_general | solution.py:48
  352.9 8.8 %convolution_add_fusion = f32[1024,2048]{1,0:T(8,128)S(1)} fusion(f32[1024,2048]{1,0:T(8,128)S(1)} %fusion.59, bf16[1024,1408]{1,0:T(8,128)(2,1)S(1)} %get-tuple-element.123, bf16[2048,1408]{1,0:T(8,128)(2,1)} %all-gather.6.cloned.1.call-done), kind=kOutput, calls=%fused_computation.16 | convolution fusion | flops 5907677184 | bytes 25427968 | tf_op jit(solution)/shard_map/dot_general | solution.py:48
  368.8 10.2 %convolution_convert_fusion.1 = bf16[2048,1408]{1,0:T(8,128)(2,1)} fusion(bf16[1024,1408]{1,0:T(8,128)(2,1)S(1)} %get-tuple-element.123, bf16[256,2048]{1,0:T(8,128)(2,1)S(1)} %copy-done.73, bf16[256,2048]{1,0:T(8,128)(2,1)S(1)} %copy-done.76, bf16[256,2048]{1,0:T(8,128)(2,1)} %collective-permute-done.20, bf16[256,2048]{1,0:T(8,128)(2,1)S(1)} %multiply_convert_fusion.3), kind=kOutput, calls=%fused_computation.5 | convolution fusion | flops 5925240832 | bytes 12845056 | tf_op jit(solution)/shard_map/dot_general | solution.py:48
  379.0 11.4 %convolution_convert_fusion.4 = bf16[1024,2048]{1,0:T(8,128)(2,1)} fusion(bf16[1024,1408]{1,0:T(8,128)(2,1)} %copy-done.82, bf16[2048,1408]{1,0:T(8,128)(2,1)} %all-gather.4.cloned.1.call-done), kind=kOutput, calls=%fused_computation.18 | convolution fusion | flops 5907677184 | bytes 12845056 | tf_op jit(solution)/shard_map/dot_general | solution.py:48
  390.4 10.2 %convolution_convert_fusion = bf16[2048,1408]{1,0:T(8,128)(2,1)} fusion(bf16[1024,1408]{1,0:T(8,128)(2,1)S(1)} %copy-done.81, bf16[256,2048]{1,0:T(8,128)(2,1)S(1)} %copy-done.74, bf16[256,2048]{1,0:T(8,128)(2,1)S(1)} %copy-done.77, bf16[256,2048]{1,0:T(8,128)(2,1)} %collective-permute-done.20, bf16[256,2048]{1,0:T(8,128)(2,1)S(1)} %multiply_convert_fusion.3), kind=kOutput, calls=%fused_computation.4 | convolution fusion | flops 5925240832 | bytes 12845056 | tf_op jit(solution)/shard_map/dot_general | solution.py:48
  400.7 12.5 %collective-permute-done.25 = bf16[256,2048]{1,0:T(8,128)(2,1)} collective-permute-done((bf16[256,2048]{1,0:T(8,128)(2,1)S(1)}, bf16[256,2048]{1,0:T(8,128)(2,1)}, u32[]{:S(2)}, u32[]{:S(2)}) %collective-permute-start.25) | collective-permute-done | bytes 1048608 | tf_op jit(solution)/shard_map/ppermute | solution.py:370
  446.8 15.3 %attention_backward.1 = (bf16[320,1024]{1,0:T(8,128)(2,1)S(1)}, bf16[2,64,1024]{2,1,0:T(8,128)(2,1)S(1)}, bf16[2,64,1024]{2,1,0:T(8,128)(2,1)S(1)}, f32[64,1]{1,0:T(8,128)S(1)}, f32[64,1]{1,0:T(8,128)S(1)}) custom-call(s32[5]{0:T(128)S(1)} %copy-done.18, f32[576,1024]{1,0:T(8,128)S(1)} %copy-done.1, f32[576,1024]{1,0:T(8,128)S(1)} %copy-done.1, ...), custom_call_target="tpu_custom_call" | custom-call | flops 1677721600 | bytes 10000000 | tf_op jit(solution)/shard_map/attention_backward/pallas_call | solution.py:244
  469.6 21.2 %collective-permute-done.30 = bf16[256,2048]{1,0:T(8,128)(2,1)S(1)} collective-permute-done((bf16[256,2048]{1,0:T(8,128)(2,1)}, bf16[256,2048]{1,0:T(8,128)(2,1)S(1)}, u32[]{:S(2)}, u32[]{:S(2)}) %collective-permute-start.30) | collective-permute-done | bytes 1048608 | tf_op jit(solution)/shard_map/ppermute | solution.py:370
  506.7 32.4 %collective-permute-done.38 = bf16[4,40,2048]{2,1,0:T(8,128)(2,1)S(1)} collective-permute-done((bf16[4,40,2048]{2,1,0:T(8,128)(2,1)S(1)}, bf16[4,40,2048]{2,1,0:T(8,128)(2,1)S(1)}, u32[]{:S(2)}, u32[]{:S(2)}) %collective-permute-start.38) | collective-permute-done | bytes 655392 | tf_op jit(solution)/shard_map/ppermute | solution.py:370
  581.6 11.8 %collective-permute-done.35 = bf16[256,576]{0,1:T(8,128)(2,1)S(1)} collective-permute-done((bf16[256,576]{0,1:T(8,128)(2,1)S(1)}, bf16[256,576]{0,1:T(8,128)(2,1)S(1)}, u32[]{:S(2)}, u32[]{:S(2)}) %collective-permute-start.35) | collective-permute-done | bytes 294944 | tf_op jit(solution)/shard_map/ppermute | solution.py:370
  610.0 10.0 %all-to-all-start.5 = ((f32[32,1,132]{2,1,0:T(1,128)}), f32[32,1,132]{2,1,0:T(1,128)S(1)}, u32[]{:S(2)}, u32[]{:S(2)}) async-start(f32[32,1,132]{2,1,0:T(1,128)} %all_to_all.30), calls=%async_computation.8 | async-start | bytes 65536 | tf_op jit(solution)/shard_map/all_to_all | solution.py:650
  (393 shorter events, 280.0 us)
Async XLA Ops:
  24.3 267.0 %all-gather.6.cloned.1.call-start = ((), (), s32[]{:S(2)}) async-start(), calls=%async_computation.10 | async-start | bytes 6488064 | tf_op jit(solution)/shard_map/all_gather | solution.py:473
  43.4 50.2 %collective-permute-start.8 = (bf16[256,2048]{1,0:T(8,128)(2,1)S(1)}, bf16[256,2048]{1,0:T(8,128)(2,1)S(1)}, u32[]{:S(2)}, u32[]{:S(2)}) collective-permute-start(bf16[256,2048]{1,0:T(8,128)(2,1)S(1)} %block_order.6), channel_id=1, source_target_pairs={{0,1},{1,0},{2,3},{3,2},{4,5},{5,4},{6,7},{7,6},{8,9},{9,8},{10,11... | collective-permute-start | bytes 3145736 | tf_op jit(solution)/shard_map/ppermute | solution.py:370
  43.5 51.1 %collective-permute-start.9 = (bf16[256,2048]{1,0:T(8,128)(2,1)}, bf16[256,2048]{1,0:T(8,128)(2,1)}, u32[]{:S(2)}, u32[]{:S(2)}) collective-permute-start(bf16[256,2048]{1,0:T(8,128)(2,1)} %collective-permute-done.1), channel_id=1, source_target_pairs={{0,1},{1,0},{2,3},{3,2},{4,5},{5,4},{6,7},{7,6},{8,9},{9,8},{10,11... | collective-permute-start | bytes 3145736 | tf_op jit(solution)/shard_map/ppermute | solution.py:370
  53.0 39.4 %collective-permute-start.4 = (bf16[256,576]{1,0:T(8,128)(2,1)S(1)}, bf16[256,576]{1,0:T(8,128)(2,1)S(1)}, u32[]{:S(2)}, u32[]{:S(2)}) collective-permute-start(bf16[256,576]{1,0:T(8,128)(2,1)S(1)} %bitcast.239), channel_id=1, source_target_pairs={{0,24},{1,25},{2,26},{3,27},{4,28},{5,29},{6,30},{7,31},{8,16},{9,... | collective-permute-start | bytes 884744 | tf_op jit(solution)/shard_map/ppermute | solution.py:370
  94.7 209.6 %all-gather.8.cloned.1.call-start = ((), (), s32[]{:S(2)}) async-start(), calls=%async_computation.11 | async-start | bytes 6488064 | tf_op jit(solution)/shard_map/all_gather | solution.py:490
  136.3 36.1 %collective-permute-start.15 = (bf16[256,1408]{1,0:T(8,128)(2,1)}, bf16[256,1408]{1,0:T(8,128)(2,1)}, u32[]{:S(2)}, u32[]{:S(2)}) collective-permute-start(bf16[256,1408]{1,0:T(8,128)(2,1)} %convert_element_type.223), channel_id=1, source_target_pairs={{0,0},{1,4},{2,2},{3,6},{4,1},{5,5},{6,3},{7,7},{8,8},{9,12},{10,1... | collective-permute-start | bytes 2162696 | tf_op jit(solution)/shard_map/ppermute | solution.py:370
  187.9 140.6 %all-gather.4.cloned.1.call-start = ((), (), s32[]{:S(2)}) async-start(), calls=%async_computation.9 | async-start | bytes 6488064 | tf_op jit(solution)/shard_map/all_gather | solution.py:505
  188.6 379.4 %reduce-scatter.4.cloned.1.call-start = ((), (), s32[]{:S(2)}) async-start(), calls=%async_computation.12 | async-start | bytes 6488064 | tf_op jit(solution)/shard_map/reduce_scatter | solution.py:539
  198.2 49.1 %collective-permute-start.18 = (bf16[256,2048]{1,0:T(8,128)(2,1)}, bf16[256,2048]{1,0:T(8,128)(2,1)S(1)}, u32[]{:S(2)}, u32[]{:S(2)}) collective-permute-start(bf16[256,2048]{1,0:T(8,128)(2,1)} %fusion.15), channel_id=1, source_target_pairs={{0,4},{1,5},{2,6},{3,7},{4,0},{5,1},{6,2},{7,3},{8,12},{9,13},{10,... | collective-permute-start | bytes 3145736 | tf_op jit(solution)/shard_map/ppermute | solution.py:370
  200.6 69.2 %collective-permute-start.19 = (bf16[256,2048]{1,0:T(8,128)(2,1)}, bf16[256,2048]{1,0:T(8,128)(2,1)S(1)}, u32[]{:S(2)}, u32[]{:S(2)}) collective-permute-start(bf16[256,2048]{1,0:T(8,128)(2,1)} %collective-permute-done.11), channel_id=1, source_target_pairs={{0,4},{1,5},{2,6},{3,7},{4,0},{5,1},{6,2},{7,3},{8,12},{9,13},{10,... | collective-permute-start | bytes 3145736 | tf_op jit(solution)/shard_map/ppermute | solution.py:370
  206.0 63.8 %collective-permute-start.22 = (bf16[256,2048]{1,0:T(8,128)(2,1)S(1)}, bf16[256,2048]{1,0:T(8,128)(2,1)S(1)}, u32[]{:S(2)}, u32[]{:S(2)}) collective-permute-start(bf16[256,2048]{1,0:T(8,128)(2,1)S(1)} %multiply_convert_fusion.3), channel_id=1, source_target_pairs={{0,6},{1,7},{2,4},{3,5},{4,2},{5,3},{6,0},{7,1},{8,14},{9,15},{10,... | collective-permute-start | bytes 3145736 | tf_op jit(solution)/shard_map/ppermute | solution.py:370
  207.8 62.0 %collective-permute-start.21 = (bf16[256,2048]{1,0:T(8,128)(2,1)S(1)}, bf16[256,2048]{1,0:T(8,128)(2,1)S(1)}, u32[]{:S(2)}, u32[]{:S(2)}) collective-permute-start(bf16[256,2048]{1,0:T(8,128)(2,1)S(1)} %multiply_convert_fusion.3), channel_id=1, source_target_pairs={{0,2},{1,3},{2,0},{3,1},{4,6},{5,7},{6,4},{7,5},{8,10},{9,11},{10,... | collective-permute-start | bytes 3145736 | tf_op jit(solution)/shard_map/ppermute | solution.py:370
  209.5 81.8 %collective-permute-start.20 = (bf16[256,2048]{1,0:T(8,128)(2,1)S(1)}, bf16[256,2048]{1,0:T(8,128)(2,1)}, u32[]{:S(2)}, u32[]{:S(2)}) collective-permute-start(bf16[256,2048]{1,0:T(8,128)(2,1)S(1)} %multiply_convert_fusion.3), channel_id=1, source_target_pairs={{0,4},{1,5},{2,6},{3,7},{4,0},{5,1},{6,2},{7,3},{8,12},{9,13},{10,... | collective-permute-start | bytes 3145736 | tf_op jit(solution)/shard_map/ppermute | solution.py:370
  328.5 239.5 %reduce-scatter.6.cloned.1.call-start = ((), (), s32[]{:S(2)}) async-start(), calls=%async_computation.13 | async-start | bytes 6488064 | tf_op jit(solution)/shard_map/reduce_scatter | solution.py:539
  365.4 35.3 %collective-permute-start.23 = (bf16[256,2048]{1,0:T(8,128)(2,1)}, bf16[256,2048]{1,0:T(8,128)(2,1)}, u32[]{:S(2)}, u32[]{:S(2)}) collective-permute-start(bf16[256,2048]{1,0:T(8,128)(2,1)} %get-tuple-element.175), channel_id=1, source_target_pairs={{0,4},{1,5},{2,6},{3,7},{4,0},{5,1},{6,2},{7,3},{8,12},{9,13},{10,... | collective-permute-start | bytes 3145736 | tf_op jit(solution)/shard_map/ppermute | solution.py:370
  367.4 45.8 %collective-permute-start.25 = (bf16[256,2048]{1,0:T(8,128)(2,1)S(1)}, bf16[256,2048]{1,0:T(8,128)(2,1)}, u32[]{:S(2)}, u32[]{:S(2)}) collective-permute-start(bf16[256,2048]{1,0:T(8,128)(2,1)S(1)} %get-tuple-element.173), channel_id=1, source_target_pairs={{0,6},{1,7},{2,4},{3,5},{4,2},{5,3},{6,0},{7,1},{8,14},{9,15},{10,... | collective-permute-start | bytes 3145736 | tf_op jit(solution)/shard_map/ppermute | solution.py:370
  429.1 176.6 %reduce-scatter.8.cloned.1.call-start = ((), (), s32[]{:S(2)}) async-start(), calls=%async_computation.14 | async-start | bytes 6488064 | tf_op jit(solution)/shard_map/reduce_scatter | solution.py:539
  442.5 49.7 %collective-permute-start.29 = (bf16[256,2048]{1,0:T(8,128)(2,1)}, bf16[256,2048]{1,0:T(8,128)(2,1)}, u32[]{:S(2)}, u32[]{:S(2)}) collective-permute-start(bf16[256,2048]{1,0:T(8,128)(2,1)} %get-tuple-element.172), channel_id=1, source_target_pairs={{0,4},{1,5},{2,6},{3,7},{4,0},{5,1},{6,2},{7,3},{8,12},{9,13},{10,... | collective-permute-start | bytes 3145736 | tf_op jit(solution)/shard_map/ppermute | solution.py:370
  443.9 46.9 %collective-permute-start.30 = (bf16[256,2048]{1,0:T(8,128)(2,1)}, bf16[256,2048]{1,0:T(8,128)(2,1)S(1)}, u32[]{:S(2)}, u32[]{:S(2)}) collective-permute-start(bf16[256,2048]{1,0:T(8,128)(2,1)} %get-tuple-element.171), channel_id=1, source_target_pairs={{0,4},{1,5},{2,6},{3,7},{4,0},{5,1},{6,2},{7,3},{8,12},{9,13},{10,... | collective-permute-start | bytes 3145736 | tf_op jit(solution)/shard_map/ppermute | solution.py:370
  446.0 49.3 %collective-permute-start.26 = (bf16[320,2048]{1,0:T(8,128)(2,1)}, bf16[320,2048]{1,0:T(8,128)(2,1)S(1)}, u32[]{:S(2)}, u32[]{:S(2)}) collective-permute-start(bf16[320,2048]{1,0:T(8,128)(2,1)} %convolution_convert_fusion.6), channel_id=1, source_target_pairs={{0,1},{1,0},{2,3},{3,2},{4,5},{5,4},{6,7},{7,6},{8,9},{9,8},{10,11... | collective-permute-start | bytes 3932168 | tf_op jit(solution)/shard_map/ppermute | solution.py:370
  497.7 62.7 %collective-permute-start.31 = (bf16[1024,576]{0,1:T(8,128)(2,1)}, bf16[1024,576]{0,1:T(8,128)(2,1)}, u32[]{:S(2)}, u32[]{:S(2)}) collective-permute-start(bf16[1024,576]{0,1:T(8,128)(2,1)} %fusion.16), channel_id=1, source_target_pairs={{0,4},{1,5},{2,6},{3,7},{4,0},{5,1},{6,2},{7,3},{8,12},{9,13},{10,... | collective-permute-start | bytes 3538952 | tf_op jit(solution)/shard_map/ppermute | solution.py:370
  499.2 39.9 %collective-permute-start.38 = (bf16[4,40,2048]{2,1,0:T(8,128)(2,1)S(1)}, bf16[4,40,2048]{2,1,0:T(8,128)(2,1)S(1)}, u32[]{:S(2)}, u32[]{:S(2)}) collective-permute-start(bf16[4,40,2048]{2,1,0:T(8,128)(2,1)S(1)} %bitcast.243), channel_id=1, source_target_pairs={{0,4},{1,5},{2,6},{3,7},{4,0},{5,1},{6,2},{7,3},{8,12},{9,13},{10,... | collective-permute-start | bytes 1966088 | tf_op jit(solution)/shard_map/ppermute | solution.py:370
  506.7 56.1 %collective-permute-start.32 = (bf16[2,256,2048]{2,1,0:T(8,128)(2,1)}, bf16[2,256,2048]{2,1,0:T(8,128)(2,1)}, u32[]{:S(2)}, u32[]{:S(2)}) collective-permute-start(bf16[2,256,2048]{2,1,0:T(8,128)(2,1)} %dynamic-slice_bitcast_fusion), channel_id=1, source_target_pairs={{0,1},{1,0},{2,3},{3,2},{4,5},{5,4},{6,7},{7,6},{8,9},{9,8},{10,11... | collective-permute-start | bytes 6291464 | tf_op jit(solution)/shard_map/ppermute | solution.py:370
  580.2 46.8 %collective-permute-start.33 = (bf16[256,2048]{1,0:T(8,128)(2,1)}, bf16[256,2048]{1,0:T(8,128)(2,1)}, u32[]{:S(2)}, u32[]{:S(2)}) collective-permute-start(bf16[256,2048]{1,0:T(8,128)(2,1)} %convert_add_fusion.3), channel_id=1, source_target_pairs={{0,2},{1,3},{2,0},{3,1},{4,6},{5,7},{6,4},{7,5},{8,10},{9,11},{10,... | collective-permute-start | bytes 3145736 | tf_op jit(solution)/shard_map/ppermute | solution.py:370
  (116 other events, 1495.9 us)
Sparse Core Ops, SparseCore 0:
  94.8 59.4 all-gather.5
  156.0 59.1 all-gather.7
  216.9 59.0 all-gather.3
  328.6 64.3 reduce-scatter.3
  413.4 64.3 reduce-scatter.5
  479.9 63.2 reduce-scatter.7
